TPU v7x, 32 devices: a whole 2x2x4 slice. The times are simulated.
32 devices in a mesh: dp: 4 (over z), tensor: 2 (over core), shard: 4 (over y, x).
Axes of the slice: x: 2, y: 2, z: 4, core: 2. Of those that a mesh axis runs over, the one named last changes fastest.
Arguments:
- weights: float32 [2, 896, 4864], P(None, 'dp', 'tensor'), may hold values from -0.1875 to 0.1875
- grads: float32 [4, 2, 896, 4864], P('dp', None, None, ('tensor', 'shard')), may hold values from -40 to 40, as said below
- bases: float32 [2, 896, 256], replicated, may hold values from -3 to 3
- first_moment: float32 [2, 256, 4864], P(None, None, ('tensor', 'shard')), may hold values from -0.12 to 0.12
- second_moment: float32 [2, 256, 4864], P(None, None, ('tensor', 'shard')), may hold values from 1e-05 to 0.001
- gain: float32 [896], replicated, may hold values from 0.5 to 1.5
- gain_grad: float32 [4, 896], P('dp'), may hold values from -384 to 384
- gain_first: float32 [896], replicated, may hold values from -3 to 3
- gain_second: float32 [896], replicated, may hold values from 0.01 to 1
Outputs:
- new_weights: float32 [2, 896, 4864], P(None, 'dp', 'tensor')
- new_bases: float32 [2, 896, 256], replicated
- new_first: float32 [2, 256, 4864], P(None, None, ('tensor', 'shard'))
- new_second: float32 [2, 256, 4864], P(None, None, ('tensor', 'shard'))
- new_gain: float32 [896], replicated
- new_gain_first: float32 [896], replicated
- new_gain_second: float32 [896], replicated
Inputs may be any that keep to these rules, and one draw needn't show every extreme that they name: `grads`: partial gradients of the data-parallel replicas.
All inputs are finite; a program needn't handle non-finite values.
Results may differ from a plain program's by a relative error of at most 0.0001.
Values sent between devices are 32-bit elements; how exact they have to be, the bound alone decides.
A program may use at most 128 MiB of HBM per device.

v0:
```python
import math

import jax
import jax.numpy as jnp
from jax import lax
from jax.sharding import PartitionSpec as P

FF = 4864
MATS = 2
NS_STEPS = 5


beta_one = 0.9
beta_two = 0.999
adam_eps = 1e-08
adam_step = 100
learn_rate = 0.02
galore_scale = 0.25
norm_eps = 1e-06


def newton_turn(newton_iterate, gram):
    return 1.5 * newton_iterate - 0.5 * jnp.einsum(
        "mdr,mrs->mds", newton_iterate, gram, precision=lax.Precision.HIGHEST
    )


def local_gram(newton_iterate):
    return jnp.einsum(
        "mdr,mds->mrs", newton_iterate, newton_iterate, precision=lax.Precision.HIGHEST
    )


def per_device(
    weights, grads, bases, first_moment, second_moment, gain, gain_grad, gain_first, gain_second
):
    highest_precision = lax.Precision.HIGHEST
    summed_gradient, gain_total = lax.psum((grads[0], gain_grad[0]), "dp")
    local_squares = jnp.sum(summed_gradient * summed_gradient)
    carried = jnp.einsum("mdf,mdr->mfr", summed_gradient, bases, precision=highest_precision)
    partial_sketch = jnp.einsum(
        "mdf,mfr->mdr", summed_gradient, carried, precision=highest_precision
    )
    sketch, all_squares = lax.psum((partial_sketch, local_squares), ("tensor", "shard"))
    frob_squares = jnp.sum(sketch * sketch, axis=(1, 2))
    newton_iterate = sketch / (jnp.sqrt(frob_squares)[:, None, None] + norm_eps)
    for ns_turn in range(NS_STEPS):
        newton_iterate = newton_turn(newton_iterate, local_gram(newton_iterate))
    total_squares = all_squares + jnp.sum(gain_total * gain_total)
    clip_factor = jnp.minimum(1.0, math.sqrt(MATS * FF) / (jnp.sqrt(total_squares) + norm_eps))
    bias_one = 1.0 - beta_one**adam_step
    bias_two = 1.0 - beta_two**adam_step
    projected_gradient = clip_factor * jnp.einsum(
        "yun,yuc->ync", newton_iterate, summed_gradient, precision=highest_precision
    )
    new_first = beta_one * first_moment + (1.0 - beta_one) * projected_gradient
    new_second = (
        beta_two * second_moment + (1.0 - beta_two) * projected_gradient * projected_gradient
    )
    update_direction = new_first / bias_one / (jnp.sqrt(new_second / bias_two) + adam_eps)
    row_count = weights.shape[1]
    row_offset = lax.axis_index("dp") * row_count
    basis_slab = lax.dynamic_slice_in_dim(newton_iterate, row_offset, row_count, 1)
    weight_delta = jnp.einsum(
        "sok,skl->sol",
        basis_slab,
        lax.all_gather(update_direction, "shard", axis=2, tiled=True),
        precision=highest_precision,
    )
    new_weights = weights - learn_rate * galore_scale * weight_delta
    clipped_gain = clip_factor * gain_total
    gain_first_new = beta_one * gain_first + (1.0 - beta_one) * clipped_gain
    gain_second_new = beta_two * gain_second + (1.0 - beta_two) * clipped_gain * clipped_gain
    gain_new = gain - learn_rate * (gain_first_new / bias_one) / (
        jnp.sqrt(gain_second_new / bias_two) + adam_eps
    )
    return (
        new_weights,
        newton_iterate,
        new_first,
        new_second,
        gain_new,
        gain_first_new,
        gain_second_new,
    )


def solution(mesh):
    placed = (
        P(None, "dp", "tensor"),
        P("dp", None, None, ("tensor", "shard")),
        P(),
        P(None, None, ("tensor", "shard")),
        P(None, None, ("tensor", "shard")),
        P(),
        P("dp", None),
        P(),
        P(),
    )
    return jax.shard_map(
        per_device,
        mesh=mesh,
        in_specs=placed,
        out_specs=(
            P(None, "dp", "tensor"),
            P(),
            P(None, None, ("tensor", "shard")),
            P(None, None, ("tensor", "shard")),
            P(),
            P(),
            P(),
        ),
        check_vma=False,
    )
```

profile of v0, /device:TPU:0, one launch (start us, length us, event | category | flops | bytes accessed | tf_op | source)
XLA Modules:
  0.0 356.5 jit_solution(18053281883207972656)
XLA Ops:
  7.2 0.0 all-reduce.3.cloned.1.call-start
  7.2 0.7 all-reduce.3.cloned.1.call-update
  7.9 0.0 all-reduce.5.cloned.1.call-start
  8.0 165.5 %all-reduce.3.cloned.1.call-done = f32[2,896,608]{1,2,0:T(8,128)} async-done(((f32[2,896,608]{1,2,0:T(8,128)}), f32[2,896,608]{1,2,0:T(8,128)}) %all-reduce.3.cloned.1.call-update) | async-done | bytes 4358160 | tf_op jit(solution)/shard_map/psum | solution.py:38
  173.4 6.1 %fusion.8 = f32[2,608,256]{2,1,0:T(8,128)S(1)} fusion(f32[2,896,608]{1,2,0:T(8,128)} %all-reduce.3.cloned.1.call-done, f32[2,896,256]{2,1,0:T(8,128)S(1)} %copy-done), kind=kOutput, calls=%fused_computation.25 | convolution fusion | flops 3347054592 | bytes 7438336 | tf_op jit(solution)/shard_map/mdf,mdr->mfr/dot_general | solution.py:40
  179.6 6.3 %convolution_bitcast_fusion = f32[2,896,256]{1,2,0:T(8,128)} fusion(f32[2,608,256]{2,1,0:T(8,128)S(1)} %fusion.8, f32[2,896,608]{1,2,0:T(8,128)S(1)} %copy-done.1), kind=kOutput, calls=%fused_computation.10 | convolution fusion | flops 3347054592 | bytes 7438336 | tf_op jit(solution)/shard_map/mdf,mfr->mdr/dot_general | solution.py:41
  186.0 0.0 all-reduce.5.cloned.1.call-update
  186.0 0.0 all-gather.2.cloned.1.call-start
  186.0 0.6 copy-done.9
  186.7 9.4 %psum.31 = f32[896]{0:T(1024)S(1)} all-reduce(f32[896]{0:T(1024)S(1)} %reduce), channel_id=1, replica_groups=mesh['dp'=4,'tensor'=2,'shard'=4] {'dp'}, use_global_device_ids=true, to_apply=%region_5.0 | all-reduce | flops 896 | bytes 7168 | tf_op jit(solution)/shard_map/psum | solution.py:38
  196.1 4.0 %multiply_reduce_fusion = f32[]{:T(128)} fusion(f32[2,896,608]{1,2,0:T(8,128)} %all-reduce.3.cloned.1.call-done), kind=kLoop, calls=%fused_computation.2 | loop fusion | flops 2179071 | bytes 4358148 | tf_op jit(solution)/shard_map/reduce_sum | solution.py:39
  200.1 0.6 multiply_reduce_fusion.2
  200.7 15.2 %psum.30 = f32[]{:T(128)} all-reduce(f32[]{:T(128)} %multiply_reduce_fusion), channel_id=1, replica_groups=mesh['dp'=4,'tensor'=2,'shard'=4] {'tensor','shard'}, use_global_device_ids=true, to_apply=%region_4.0 | all-reduce | flops 1 | bytes 8 | tf_op jit(solution)/shard_map/psum | solution.py:44
  217.3 28.1 %all-reduce.5.cloned.1.call-done = f32[2,896,256]{1,2,0:T(8,128)} async-done(((f32[2,896,256]{1,2,0:T(8,128)}), f32[2,896,256]{1,2,0:T(8,128)}) %all-reduce.5.cloned.1.call-update) | async-done | bytes 1835024 | tf_op jit(solution)/shard_map/psum | solution.py:44
  245.4 2.0 multiply_reduce_fusion.1
  247.3 0.1 copy-done.3
  247.4 2.2 fusion.3
  249.6 2.3 multiply_subtract_fusion.4
  252.0 2.0 fusion.9
  254.0 2.1 multiply_subtract_fusion.3
  256.1 2.0 fusion.10
  258.2 2.4 multiply_subtract_fusion.2
  260.5 2.0 fusion.11
  262.6 2.1 multiply_subtract_fusion.1
  264.7 2.0 fusion.12
  266.8 2.1 multiply_subtract_fusion
  269.0 7.3 %add_divide_fusion = (f32[2,256,608]{1,2,0:T(8,128)}, f32[2,256,608]{1,2,0:T(8,128)}, f32[2,256,608]{1,2,0:T(8,128)}) fusion(f32[2,256,608]{1,2,0:T(8,128)S(1)} %copy-done.4, f32[2,256,608]{1,2,0:T(8,128)S(1)} %copy-done.5, f32[2,896,256]{1,2,0:T(8,128)S(1)} %multiply_subtract_fusion, f32[2,896,608]{1,2,0:T(8,128)S(1)} %bitcast.28, f32[]{:T(128)S(6)} %min_shard_map.3), kind=kOutput, calls=%fused_computation.13 | convolution fusion | flops 3350790144 | bytes 12419076 | tf_op jit(solution)/shard_map/yun,yuc->ync/dot_general | solution.py:53
  276.3 0.0 all-gather.2.cloned.1.call-update
  276.4 0.6 divide_subtract_fusion
  277.0 2.7 copy.28
  279.7 55.3 %all-gather.2.cloned.1.call-done = f32[2,256,2432]{1,2,0:T(8,128)} async-done(((f32[2,256,608]{1,2,0:T(8,128)}), f32[2,256,2432]{1,2,0:T(8,128)}) %all-gather.2.cloned.1.call-update) | async-done | bytes 4980752 | tf_op jit(solution)/shard_map/all_gather | solution.py:67
  335.0 14.5 %fusion = f32[2,224,2432]{2,1,0:T(8,128)} fusion(f32[2,224,2432]{2,1,0:T(8,128)} %param.9, f32[2,256,2432]{1,2,0:T(8,128)} %all-gather.2.cloned.1.call-done, f32[2,896,256]{1,2,0:T(8,128)} %copy-done.2, s32[]{:T(128)S(6)} %select_n.3), kind=kOutput, calls=%fused_computation.1 | convolution fusion | flops 3349233664 | bytes 14221316 | tf_op jit(solution)/shard_map/sok,skl->sol/dot_general | solution.py:64
  (25 shorter events, 0.1 us)
Async XLA Ops:
  7.2 166.3 %copy-start = (f32[2,896,256]{2,1,0:T(8,128)S(1)}, f32[2,896,256]{2,1,0:T(8,128)}, u32[]{:S(2)}) copy-start(f32[2,896,256]{2,1,0:T(8,128)} %param.11) | copy-start | bytes 5505028
  7.2 166.2 %all-reduce.3.cloned.1.call-start = ((), (), s32[]{:S(2)}) async-start(), calls=%async_computation | async-start | bytes 8716288 | tf_op jit(solution)/shard_map/psum | solution.py:38
  7.9 237.4 %all-reduce.5.cloned.1.call-start = ((), (), s32[]{:S(2)}) async-start(), calls=%async_computation.1 | async-start | bytes 3670016 | tf_op jit(solution)/shard_map/psum | solution.py:44
  173.4 6.2 %copy-start.1 = (f32[2,896,608]{1,2,0:T(8,128)S(1)}, f32[2,896,608]{1,2,0:T(8,128)}, u32[]{:S(2)}) copy-start(f32[2,896,608]{1,2,0:T(8,128)} %all-reduce.3.cloned.1.call-done) | copy-start | bytes 13074436
  186.0 0.7 copy-start.9
  186.0 149.0 %all-gather.2.cloned.1.call-start = ((), (), s32[]{:S(2)}) async-start(), calls=%async_computation.2 | async-start | bytes 6225920 | tf_op jit(solution)/shard_map/all_gather | solution.py:67
  245.4 2.1 copy-start.3
  262.6 6.4 %slice-start = ((s8[4358144]{0:T(1024)(128)(4,1)}), s8[4194304]{0:T(1024)(128)(4,1)S(1)}, s32[]{:S(2)}) async-start(s8[4358144]{0:T(1024)(128)(4,1)} %bitcast.27), calls=%async_computation.3 | async-start | bytes 8388608
  264.7 4.2 %slice-start.1 = ((s8[4358144]{0:T(1024)(128)(4,1)}), s8[163840]{0:T(1024)(128)(4,1)S(1)}, s32[]{:S(2)}) async-start(s8[4358144]{0:T(1024)(128)(4,1)} %bitcast.27), calls=%async_computation.4 | async-start | bytes 327680
  266.8 2.2 copy-start.4
  266.8 2.2 copy-start.5
  269.0 7.3 %copy-start.2 = (f32[2,896,256]{1,2,0:T(8,128)}, f32[2,896,256]{1,2,0:T(8,128)S(1)}, u32[]{:S(2)}) copy-start(f32[2,896,256]{1,2,0:T(8,128)S(1)} %multiply_subtract_fusion) | copy-start | bytes 5505028
  269.0 7.3 %copy-start.6 = (f32[896]{0:T(1024)S(1)}, f32[896]{0:T(1024)}, u32[]{:S(2)}) copy-start(f32[896]{0:T(1024)} %param.14) | copy-start | bytes 10756
  269.0 7.3 %copy-start.7 = (f32[896]{0:T(1024)S(1)}, f32[896]{0:T(1024)}, u32[]{:S(2)}) copy-start(f32[896]{0:T(1024)} %param.16) | copy-start | bytes 10756
  269.0 7.3 %copy-start.8 = (f32[896]{0:T(1024)S(1)}, f32[896]{0:T(1024)}, u32[]{:S(2)}) copy-start(f32[896]{0:T(1024)} %param.17) | copy-start | bytes 10756
Sparse Core Ops, SparseCore 0:
  10.4 162.9 all-reduce.2
  186.1 59.2 all-reduce.4
  276.4 58.5 all-gather.1
where the time goes:
time: 363 us; the launch traced here: 357 us
  waiting for transfers between devices  250 us (69%)
  matrix products  55.7 us (15%)
  blocking collectives  24.6 us (7%)
  between operations  15.8 us (4%)
  other arithmetic  7.19 us (2%)
    psum x1, waiting for transfers between devices, per_device(): summed_gradient, gain_total = lax.psum((grads[0], gain_grad[0]), 'dp')  165 us
    all_gather x1, waiting for transfers between devices, per_device(): lax.all_gather(update_direction, 'shard', axis=2, tiled=True)  55.3 us
    psum x1, waiting for transfers between devices, per_device(): lax.psum((partial_sketch, local_squares), ('tensor', 'shard'))  28.1 us
    psum x1, blocking collectives, per_device(): lax.psum((partial_sketch, local_squares), ('tensor', 'shard'))  15.2 us
    dot_general x1, matrix products, per_device(): jnp.einsum('sok,skl->sol', basis_slab, lax.all_gather(update_direction, '...  14.5 us
    dot_general x5, matrix products, newton_turn(): jnp.einsum('mdr,mrs->mds', newton_iterate, gram, precision=lax.Precision....  11.1 us
    dot_general x5, matrix products, local_gram(): jnp.einsum('mdr,mds->mrs', newton_iterate, newton_iterate, precision=lax....  10.3 us
    psum x1, blocking collectives, per_device(): summed_gradient, gain_total = lax.psum((grads[0], gain_grad[0]), 'dp')  9.44 us
  transfers between devices with their start and end apart: 3, of which 3 were waited for; matrix products, arithmetic and copies ran while one was open for 2% of the time, Pallas kernels for 0%

commit v1 on v0

v1 whole, which is shorter than its diff:
```python
import functools
import math

import jax
import jax.numpy as jnp
from jax import lax
from jax.experimental import pallas as pl
from jax.experimental.pallas import tpu as pltpu
from jax.sharding import PartitionSpec as P

NS_STEPS = 5
MATS = 2

beta_one = 0.9
beta_two = 0.999
adam_eps = 1e-08
adam_step = 100
learn_rate = 0.02
galore_scale = 0.25
norm_eps = 1e-06

MESH = pl.DeviceIdType.MESH
VMEM = pl.BlockSpec(memory_space=pltpu.VMEM)
SKEW = 2


def dot(left, right, dims, precision=lax.Precision.HIGH):
    return lax.dot_general(
        left, right, (dims, ((), ())), precision=precision, preferred_element_type=jnp.float32
    )


def greet_line(dp, z):
    barrier = pltpu.get_barrier_semaphore()
    for k in range(1, dp):
        pl.semaphore_signal(
            barrier, inc=1, device_id={"dp": lax.rem(z + k, dp)}, device_id_type=MESH
        )
    pl.semaphore_wait(barrier, dp - 1)


def chunk_rows(rows, want):
    best = 8
    for size in range(8, want + 1, 8):
        if rows % size == 0:
            best = size
    return best


def line_sum_kernel(
    dp, ch, g_ref, gain_ref, out_ref, gain_out, rbuf, gbuf, send, recv, gsend, grecv
):
    z = lax.axis_index("dp")
    nch = g_ref.shape[1] // ch
    greet_line(dp, z)

    def remote(m, c, src, target):
        rows = pl.ds(c * ch, ch)
        return pltpu.make_async_remote_copy(
            src_ref=src.at[m, rows],
            dst_ref=rbuf.at[m, rows],
            send_sem=send.at[m, c],
            recv_sem=recv.at[m, c],
            device_id={"dp": target},
            device_id_type=MESH,
        )

    hops = (dp - 1 - z, z)
    target = (jnp.maximum(z - 1, 0), jnp.minimum(z + 1, dp - 1))

    def step(i, carry):
        for m in range(MATS):
            c = i - SKEW * hops[m]
            live = jnp.logical_and(c >= 0, c < nch)
            rows = pl.ds(pl.multiple_of(c * ch, 8), ch)

            @pl.when(jnp.logical_and(live, hops[m] == 0))
            def _():
                remote(m, c, g_ref, target[m]).start()

            @pl.when(jnp.logical_and(live, hops[m] > 0))
            def _():
                remote(m, c, rbuf, target[m]).wait_recv()

            @pl.when(jnp.logical_and(live, jnp.logical_and(hops[m] > 0, hops[m] < dp - 1)))
            def _():
                rbuf[m, rows, :] = rbuf[m, rows, :] + g_ref[m, rows, :]
                remote(m, c, rbuf, target[m]).start()

            @pl.when(jnp.logical_and(live, hops[m] == dp - 1))
            def _():
                out_ref[rows, :] = rbuf[m, rows, :] + g_ref[m, rows, :]

        return carry

    gcopies = []
    for k in range(1, dp):
        copy = pltpu.make_async_remote_copy(
            src_ref=gain_ref,
            dst_ref=gbuf.at[k],
            send_sem=gsend.at[k],
            recv_sem=grecv.at[k],
            device_id={"dp": lax.rem(z + k, dp)},
            device_id_type=MESH,
        )
        copy.start()
        gcopies.append(copy)

    lax.fori_loop(0, nch + SKEW * (dp - 1), step, 0)

    total = gain_ref[...]
    for k in range(1, dp):
        gcopies[k - 1].wait()
        total = total + gbuf[k]
    gain_out[...] = total

    @pl.when(jnp.logical_and(z > 0, z < dp - 1))
    def _():
        out_ref[...] = jnp.zeros_like(out_ref)

    def drain(c, carry):
        for m in range(MATS):

            @pl.when(hops[m] < dp - 1)
            def _():
                remote(m, c, rbuf, target[m]).wait_send()

        return carry

    lax.fori_loop(0, nch, drain, 0)


def line_sum(dp, grads, gain_grad):
    mats, rows, cols = grads.shape
    ch = chunk_rows(rows, 32)
    nch = rows // ch
    dma = pltpu.SemaphoreType.DMA
    return pl.pallas_call(
        functools.partial(line_sum_kernel, dp, ch),
        out_shape=(
            jax.ShapeDtypeStruct((rows, cols), jnp.float32),
            jax.ShapeDtypeStruct(gain_grad.shape, jnp.float32),
        ),
        in_specs=[VMEM, VMEM],
        out_specs=(VMEM, VMEM),
        scratch_shapes=[
            pltpu.VMEM((mats, rows, cols), jnp.float32),
            pltpu.VMEM((dp,) + gain_grad.shape, jnp.float32),
            dma((mats, nch)),
            dma((mats, nch)),
            dma((dp,)),
            dma((dp,)),
        ],
        compiler_params=pltpu.CompilerParams(
            collective_id=0, has_side_effects=True, vmem_limit_bytes=40 * 2**20
        ),
    )(grads, gain_grad)


def line_spread_kernel(dp, parts, *refs):
    n = len(parts)
    ins, outs = refs[:n], refs[n : 2 * n]
    send, recv, keep = refs[2 * n :]
    z = lax.axis_index("dp")
    greet_line(dp, z)
    hops = (z, dp - 1 - z)
    target = (jnp.minimum(z + 1, dp - 1), jnp.maximum(z - 1, 0))
    plan = [(a, r, ch) for a, (rows, ch) in enumerate(parts) for r in range(0, rows, ch)]

    def remote(m, k, first):
        a, r, ch = plan[k]
        dst = outs[a].at[m, pl.ds(r, ch)]
        return pltpu.make_async_remote_copy(
            src_ref=ins[a].at[pl.ds(r, ch)] if first else dst,
            dst_ref=dst,
            send_sem=send.at[m, k],
            recv_sem=recv.at[m, k],
            device_id={"dp": target[m]},
            device_id_type=MESH,
        )

    for m in range(MATS):

        @pl.when(hops[m] == 0)
        def _():
            for k in range(len(plan)):
                remote(m, k, True).start()
            for a in range(n):
                pltpu.make_async_copy(ins[a], outs[a].at[m], keep.at[a]).start()

    for i in range(len(plan) + SKEW * (dp - 1)):
        for m in range(MATS):
            for h in range(1, dp):
                k = i - SKEW * h
                if 0 <= k < len(plan):

                    @pl.when(hops[m] == h)
                    def _():
                        remote(m, k, False).wait_recv()
                        if h < dp - 1:
                            remote(m, k, False).start()

    for m in range(MATS):

        @pl.when(hops[m] == 0)
        def _():
            for a in range(n):
                pltpu.make_async_copy(ins[a], outs[a].at[m], keep.at[a]).wait()

        @pl.when(hops[m] < dp - 1)
        def _():
            for k in range(len(plan)):
                remote(m, k, False).wait_send()


def line_spread(dp, arrays, counts):
    parts = tuple((a.shape[0], a.shape[0] // c) for a, c in zip(arrays, counts))
    nk = sum(counts)
    dma = pltpu.SemaphoreType.DMA
    return pl.pallas_call(
        functools.partial(line_spread_kernel, dp, parts),
        out_shape=tuple(jax.ShapeDtypeStruct((MATS,) + a.shape, jnp.float32) for a in arrays),
        in_specs=[VMEM] * len(arrays),
        out_specs=tuple(VMEM for _ in arrays),
        scratch_shapes=[dma((MATS, nk)), dma((MATS, nk)), dma((len(arrays),))],
        compiler_params=pltpu.CompilerParams(
            collective_id=1, has_side_effects=True, vmem_limit_bytes=32 * 2**20
        ),
    )(*arrays)


def per_device(
    dp,
    weights,
    grads,
    bases,
    first_moment,
    second_moment,
    gain,
    gain_grad,
    gain_first,
    gain_second,
):
    z = lax.axis_index("dp")
    ff = first_moment.shape[2] * lax.axis_size(("tensor", "shard"))
    mine, gain_total = line_sum(dp, grads[0], gain_grad)
    gain_total = gain_total[0]
    basis = lax.dynamic_index_in_dim(bases, jnp.where(z * 2 >= dp, 1, 0), 0, keepdims=False)
    rows, rank = basis.shape
    local_squares = jnp.sum(mine * mine)
    carried = dot(mine, basis, ((0,), (0,)))
    partial = dot(mine, carried, ((1,), (0,)))
    packed = jnp.concatenate(
        [partial, jnp.full((8, rank), local_squares, jnp.float32)], axis=0
    )
    packed = lax.psum(packed, ("tensor", "shard"))
    sketch, squares = packed[:rows], packed[rows:, :128]
    iterate = sketch / (jnp.sqrt(jnp.sum(sketch * sketch)) + norm_eps)
    gram = dot(iterate, iterate, ((0,), (0,)))
    eye = jnp.eye(rank, dtype=jnp.float32)
    product = None
    for turn in range(NS_STEPS):
        factor = 1.5 * eye - 0.5 * gram
        product = factor if product is None else dot(product, factor, ((1,), (0,)))
        if turn < NS_STEPS - 1:
            gram = dot(dot(factor, gram, ((1,), (0,))), factor, ((1,), (0,)))
    new_basis = dot(iterate, product, ((1,), (0,)))
    projected = dot(new_basis, mine, ((0,), (0,)))
    projected, squares, new_bases = line_spread(dp, (projected, squares, new_basis), (8, 1, 7))

    total_squares = squares[0, 0, 0] + squares[1, 0, 0] + jnp.sum(gain_total * gain_total)
    clip_factor = jnp.minimum(1.0, math.sqrt(MATS * ff) / (jnp.sqrt(total_squares) + norm_eps))
    bias_one = 1.0 - beta_one**adam_step
    bias_two = 1.0 - beta_two**adam_step
    projected_gradient = clip_factor * projected
    new_first = beta_one * first_moment + (1.0 - beta_one) * projected_gradient
    new_second = (
        beta_two * second_moment + (1.0 - beta_two) * projected_gradient * projected_gradient
    )
    direction = new_first / bias_one / (jnp.sqrt(new_second / bias_two) + adam_eps)
    row_count = weights.shape[1]
    slab = lax.dynamic_slice_in_dim(new_bases, z * row_count, row_count, 1)
    delta = lax.dot_general(
        slab,
        direction,
        (((2,), (1,)), ((0,), (0,))),
        precision=lax.Precision.HIGH,
        preferred_element_type=jnp.float32,
    )
    delta = lax.all_gather(delta, "shard", axis=2, tiled=True)
    new_weights = weights - learn_rate * galore_scale * delta
    clipped_gain = clip_factor * gain_total
    gain_first_new = beta_one * gain_first + (1.0 - beta_one) * clipped_gain
    gain_second_new = beta_two * gain_second + (1.0 - beta_two) * clipped_gain * clipped_gain
    gain_new = gain - learn_rate * (gain_first_new / bias_one) / (
        jnp.sqrt(gain_second_new / bias_two) + adam_eps
    )
    return (
        new_weights,
        new_bases,
        new_first,
        new_second,
        gain_new,
        gain_first_new,
        gain_second_new,
    )


def solution(mesh):
    placed = (
        P(None, "dp", "tensor"),
        P("dp", None, None, ("tensor", "shard")),
        P(),
        P(None, None, ("tensor", "shard")),
        P(None, None, ("tensor", "shard")),
        P(),
        P("dp", None),
        P(),
        P(),
    )
    return jax.shard_map(
        functools.partial(per_device, mesh.shape["dp"]),
        mesh=mesh,
        in_specs=placed,
        out_specs=(
            P(None, "dp", "tensor"),
            P(),
            P(None, None, ("tensor", "shard")),
            P(None, None, ("tensor", "shard")),
            P(),
            P(),
            P(),
        ),
        check_vma=False,
    )
```

time: 363 us -> 305 us (0.84); the launches traced: 357 us -> 304 us
  waiting for transfers between devices: 250 us -> 95 us
  Pallas kernels: 0 us -> 115 us
  local copies, waits for them, and re-layouts: 3.46 us -> 45.6 us
  matrix products: 55.7 us -> 15.3 us
  blocking collectives: 24.6 us -> 0 us
  other arithmetic: 7.19 us -> 15.6 us
    psum x2 -> x1, waiting for transfers between devices: 194 us -> 51.4 us  [per_device(): packed = lax.psum(packed, ('tensor', 'shard'))]
    pallas_call x0 -> x2, Pallas kernels: none -> 115 us  [the longest x1 66.6 us: line_sum(): pl.pallas_call(functools.partial(line_sum_kernel, dp, ch), out_shape=(jax...]
    dot_general x14 -> x18, matrix products: 55.7 us -> 15.3 us  [the longest x17 12.9 us: dot(): lax.dot_general(left, right, (dims, ((), ())), precision=precision, prefe...]
    unnamed x25 -> x38, local copies, waits for them, and re-layouts: 3.46 us -> 41.9 us
    psum x2 -> x0, blocking collectives: 24.6 us -> none  [the longest x1 15.2 us: per_device(): lax.psum((partial_sketch, local_squares), ('tensor', 'shard'))]
    all_gather x1, waiting for transfers between devices: 55.3 us -> 43.5 us  [per_device(): delta = lax.all_gather(delta, 'shard', axis=2, tiled=True)]
    sub x0 -> x1, other arithmetic: none -> 8.99 us  [per_device(): new_weights = weights - learn_rate * galore_scale * delta]
  transfers between devices with their start and end apart: 3 -> 2, of which waited for: 3 -> 2; matrix products, arithmetic and copies ran while one was open for 2% -> 6% of each run, Pallas kernels for 0% -> 0%
where the time goes in v1:
time: 305 us; the launch traced here: 304 us
  Pallas kernels  115 us (38%)
  waiting for transfers between devices  95 us (31%)
  local copies, waits for them, and re-layouts  45.6 us (15%)
  between operations  17.1 us (6%)
  other arithmetic  15.6 us (5%)
  matrix products  15.3 us (5%)
    pallas_call x1, Pallas kernels, line_sum(): pl.pallas_call(functools.partial(line_sum_kernel, dp, ch), out_shape=(jax...  66.6 us
    psum x1, waiting for transfers between devices, per_device(): packed = lax.psum(packed, ('tensor', 'shard'))  51.4 us
    pallas_call x1, Pallas kernels, line_spread(): pl.pallas_call(functools.partial(line_spread_kernel, dp, parts), out_shap...  48.4 us
    all_gather x1, waiting for transfers between devices, per_device(): delta = lax.all_gather(delta, 'shard', axis=2, tiled=True)  43.5 us
    unnamed x38, local copies, waits for them, and re-layouts  41.9 us
    dot_general x17, matrix products, dot(): lax.dot_general(left, right, (dims, ((), ())), precision=precision, prefe...  12.9 us
    sub x1, other arithmetic, per_device(): new_weights = weights - learn_rate * galore_scale * delta  8.99 us
  transfers between devices with their start and end apart: 2, of which 2 were waited for; matrix products, arithmetic and copies ran while one was open for 6% of the time, Pallas kernels for 0%

profile of v1, /device:TPU:0, one launch (start us, length us, event | category | flops | bytes accessed | tf_op | source)
XLA Modules:
  0.0 303.7 jit_solution(5620283960445006256)
XLA Ops:
  7.2 5.8 %copy.23 = f32[1,2,896,608]{3,2,1,0:T(8,128)} copy(f32[1,2,896,608]{2,3,1,0:T(8,128)} %param.10) | data formatting | bytes 8716288 | tf_op args[1]
  13.0 2.3 copy-done.4
  15.3 66.6 %shard_map.144 = (f32[896,608]{1,0:T(8,128)S(1)}, f32[1,896]{1,0:T(1,128)S(1)}) custom-call(f32[2,896,608]{2,1,0:T(8,128)S(1)} %bitcast.23, f32[1,896]{1,0:T(1,128)S(1)} %copy-done.6), custom_call_target="tpu_custom_call" | custom-call | tf_op jit(solution)/shard_map/pallas_call | solution.py:138
  82.0 1.4 copy-done.1
  83.3 1.2 multiply_reduce_fusion
  84.5 3.8 %fusion.8 = f32[608,256]{1,0:T(8,128)S(1)} fusion(f32[896,608]{1,0:T(8,128)} %copy-done.1, f32[2,896,256]{2,1,0:T(8,128)S(1)} %copy-done, s32[]{:T(128)S(6)} %select_n.9), kind=kOutput, calls=%fused_computation.13 | convolution fusion | flops 836763648 | bytes 3719172 | tf_op jit(solution)/shard_map/dot_general | solution.py:28
  88.3 1.3 fusion.101
  89.6 1.7 concatenate.3
  91.4 1.5 copy.25
  92.9 2.8 copy.26
  95.6 0.6 multiply_reduce_fusion.3
  96.3 51.4 %all-reduce.3.cloned.1.call-done = f32[904,256]{1,0:T(8,128)} async-done(((f32[904,256]{1,0:T(8,128)}), f32[904,256]{1,0:T(8,128)}) %all-reduce.3.cloned.1.call-update) | async-done | bytes 925712 | tf_op jit(solution)/shard_map/psum | solution.py:256
  147.7 2.0 multiply_reduce_fusion.1
  150.4 2.4 fusion.16
  156.6 0.5 fusion.15.refs_2_
  157.2 1.1 copy-done.3
  158.3 1.5 fusion.103.refs_0_
  159.8 48.4 %shard_map.145 = (f32[2,256,608]{2,1,0:T(8,128)S(1)}, f32[2,8,128]{2,1,0:T(8,128)S(1)}, f32[2,896,256]{2,1,0:T(8,128)S(1)}) custom-call(f32[256,608]{1,0:T(8,128)S(1)} %fusion.103.refs_0_, f32[8,128]{1,0:T(8,128)S(1)} %slice.17.refs_1_, f32[896,256]{1,0:T(8,128)S(1)} %fusion.15.refs_2_), custom_call_target="tpu_custom_call" | custom-call | tf_op jit(solution)/shard_map/pallas_call | solution.py:220
  208.3 1.2 copy-done.5
  209.5 0.5 fusion.100
  212.0 2.2 multiply_add_fusion
  214.3 1.0 copy-done.7
  215.7 2.4 fusion.1
  218.1 1.5 copy.28
  219.6 8.6 %copy.29 = f32[2,224,2432]{1,0,2:T(2,128)} copy(f32[2,224,2432]{2,1,0:T(8,128)} %param.9) | data formatting | bytes 8716288 | tf_op args[0]
  228.2 2.8 copy.31
  231.1 1.4 copy.32
  232.6 0.6 divide_subtract_fusion
  233.2 43.5 %all-gather.2.cloned.1.call-done = f32[2,224,2432]{1,0,2:T(2,128)} async-done(((f32[2,224,608]{1,0,2:T(2,128)}), f32[2,224,2432]{1,0,2:T(2,128)}) %all-gather.2.cloned.1.call-update) | async-done | bytes 4358160 | tf_op jit(solution)/shard_map/all_gather | solution.py:290
  276.7 9.0 %multiply_subtract_fusion = f32[2,224,2432]{1,0,2:T(2,128)} fusion(f32[2,224,2432]{1,0,2:T(2,128)} %copy.29, f32[2,224,2432]{1,0,2:T(2,128)} %all-gather.2.cloned.1.call-done), kind=kLoop, calls=%fused_computation | loop fusion | flops 2179072 | bytes 13074432 | tf_op jit(solution)/shard_map/sub | solution.py:291
  285.7 8.3 %copy.30 = f32[2,224,2432]{2,1,0:T(8,128)} copy(f32[2,224,2432]{1,0,2:T(2,128)} %multiply_subtract_fusion) | data formatting | bytes 8716288
  294.0 2.8 copy.37
  (43 shorter events, 4.4 us)
Async XLA Ops:
  7.2 77.3 %copy-start = (f32[2,896,256]{2,1,0:T(8,128)S(1)}, f32[2,896,256]{2,1,0:T(8,128)}, u32[]{:S(2)}) copy-start(f32[2,896,256]{2,1,0:T(8,128)} %param.11) | copy-start | bytes 5505028
  7.2 140.5 %all-reduce.3.cloned.1.call-start = ((), (), s32[]{:S(2)}) async-start(), calls=%async_computation | async-start | bytes 1851392 | tf_op jit(solution)/shard_map/psum | solution.py:256
  7.2 5.8 %copy-start.6 = (f32[1,896]{1,0:T(1,128)S(1)}, f32[1,896]{1,0:T(1,128)}, u32[]{:S(2)}) copy-start(f32[1,896]{1,0:T(1,128)} %gain_ref.1) | copy-start | bytes 10756
  13.0 2.3 copy-start.4
  81.9 1.4 copy-start.1
  84.5 3.8 %copy-start.2 = (f32[896,608]{1,0:T(8,128)S(1)}, f32[896,608]{1,0:T(8,128)}, u32[]{:S(2)}) copy-start(f32[896,608]{1,0:T(8,128)} %copy-done.1) | copy-start | bytes 6537220
  89.6 1.8 copy-start.10
  91.3 185.4 %all-gather.2.cloned.1.call-start = ((), (), s32[]{:S(2)}) async-start(), calls=%async_computation.1 | async-start | bytes 6225920 | tf_op jit(solution)/shard_map/all_gather | solution.py:290
  155.4 1.2 copy-start.11
  156.6 1.6 copy-start.3
  208.2 1.2 copy-start.5
  214.2 1.1 copy-start.7
  214.2 1.5 copy-start.9
  228.2 2.9 copy-start.8
  231.1 1.5 copy-start.12
  231.1 1.5 copy-start.13
  231.1 1.5 copy-start.14
Sparse Core Ops, SparseCore 0:
  91.5 56.1 all-reduce.2
  219.8 56.9 all-gather.1

commit v2 on v1

--- a/solution.py
+++ b/solution.py
@@ -97,7 +97,7 @@
     for k in range(1, dp):
         copy = pltpu.make_async_remote_copy(
             src_ref=gain_ref,
-            dst_ref=gbuf.at[k],
+            dst_ref=gbuf.at[z],
             send_sem=gsend.at[k],
             recv_sem=grecv.at[k],
             device_id={"dp": lax.rem(z + k, dp)},
@@ -108,11 +108,10 @@
 
     lax.fori_loop(0, nch + SKEW * (dp - 1), step, 0)
 
-    total = gain_ref[...]
-    for k in range(1, dp):
-        gcopies[k - 1].wait()
-        total = total + gbuf[k]
-    gain_out[...] = total
+    for copy in gcopies:
+        copy.wait()
+    gbuf[pl.ds(z, 1)] = gain_ref[...][None]
+    gain_out[...] = jnp.sum(gbuf[...], axis=0)
 
     @pl.when(jnp.logical_and(z > 0, z < dp - 1))
     def _():
@@ -160,18 +159,34 @@
 def line_spread_kernel(dp, parts, *refs):
     n = len(parts)
     ins, outs = refs[:n], refs[n : 2 * n]
-    send, recv, keep = refs[2 * n :]
-    z = lax.axis_index("dp")
-    greet_line(dp, z)
+    send, recv, keep, pair_send, pair_recv = refs[2 * n :]
+    z, core = lax.axis_index("dp"), lax.axis_index("tensor")
+    barrier = pltpu.get_barrier_semaphore()
+    for k in range(1, dp):
+        pl.semaphore_signal(
+            barrier, inc=1, device_id={"dp": lax.rem(z + k, dp)}, device_id_type=MESH
+        )
+    pl.semaphore_signal(barrier, inc=1, device_id={"tensor": 1 - core}, device_id_type=MESH)
+    pl.semaphore_wait(barrier, dp)
     hops = (z, dp - 1 - z)
     target = (jnp.minimum(z + 1, dp - 1), jnp.maximum(z - 1, 0))
-    plan = [(a, r, ch) for a, (rows, ch) in enumerate(parts) for r in range(0, rows, ch)]
+    plan = []
+    for a, (rows, ch) in enumerate(parts):
+        span = rows // 2 if a == n - 1 else rows
+        plan += [(a, r, ch, span) for r in range(0, span, ch)]
+
+    def rows_of(k, owner):
+        a, r, ch, span = plan[k]
+        if a < n - 1:
+            return pl.ds(r, ch)
+        return pl.ds(pl.multiple_of(owner * span + r, 8), ch)
 
     def remote(m, k, first):
-        a, r, ch = plan[k]
-        dst = outs[a].at[m, pl.ds(r, ch)]
+        a = plan[k][0]
+        rows = rows_of(k, core)
+        dst = outs[a].at[m, rows]
         return pltpu.make_async_remote_copy(
-            src_ref=ins[a].at[pl.ds(r, ch)] if first else dst,
+            src_ref=ins[a].at[rows] if first else dst,
             dst_ref=dst,
             send_sem=send.at[m, k],
             recv_sem=recv.at[m, k],
@@ -179,6 +194,18 @@
             device_id_type=MESH,
         )
 
+    def across(m, k, owner):
+        ref = outs[n - 1].at[m, rows_of(k, owner)]
+        return pltpu.make_async_remote_copy(
+            src_ref=ref,
+            dst_ref=ref,
+            send_sem=pair_send.at[m, k],
+            recv_sem=pair_recv.at[m, k],
+            device_id={"tensor": 1 - core},
+            device_id_type=MESH,
+        )
+
+    split = [k for k in range(len(plan)) if plan[k][0] == n - 1]
     for m in range(MATS):
 
         @pl.when(hops[m] == 0)
@@ -199,6 +226,8 @@
                         remote(m, k, False).wait_recv()
                         if h < dp - 1:
                             remote(m, k, False).start()
+                        if k in split:
+                            across(m, k, core).start()
 
     for m in range(MATS):
 
@@ -207,26 +236,238 @@
             for a in range(n):
                 pltpu.make_async_copy(ins[a], outs[a].at[m], keep.at[a]).wait()
 
+        @pl.when(hops[m] > 0)
+        def _():
+            for k in split:
+                across(m, k, core).wait_send()
+                across(m, k, 1 - core).wait_recv()
+
         @pl.when(hops[m] < dp - 1)
         def _():
             for k in range(len(plan)):
                 remote(m, k, False).wait_send()
 
 
-def line_spread(dp, arrays, counts):
-    parts = tuple((a.shape[0], a.shape[0] // c) for a, c in zip(arrays, counts))
-    nk = sum(counts)
+def line_spread(dp, arrays, sizes):
+    parts = tuple((a.shape[0], size) for a, size in zip(arrays, sizes))
+    nk = sum(a.shape[0] // size for a, size in zip(arrays, sizes))
     dma = pltpu.SemaphoreType.DMA
     return pl.pallas_call(
         functools.partial(line_spread_kernel, dp, parts),
         out_shape=tuple(jax.ShapeDtypeStruct((MATS,) + a.shape, jnp.float32) for a in arrays),
         in_specs=[VMEM] * len(arrays),
         out_specs=tuple(VMEM for _ in arrays),
-        scratch_shapes=[dma((MATS, nk)), dma((MATS, nk)), dma((len(arrays),))],
+        scratch_shapes=[dma((MATS, nk))] * 2 + [dma((len(arrays),))] + [dma((MATS, nk))] * 2,
         compiler_params=pltpu.CompilerParams(
             collective_id=1, has_side_effects=True, vmem_limit_bytes=32 * 2**20
         ),
     )(*arrays)
+
+
+def plane_sum_kernel(
+    x_ref, sq_ref, out_ref, sq_out, abuf, hbuf, bbuf, sqbuf, a_sem, b_sem, c_sem, d_sem, s_sem
+):
+    core, s = lax.axis_index("tensor"), lax.axis_index("shard")
+    half = x_ref.shape[0] // 2
+    piece = half // 4
+    barrier = pltpu.get_barrier_semaphore()
+    others = [(lax.rem(core + i, 2), lax.rem(s + k, 4)) for i in range(2) for k in range(4)][1:]
+    for c, t in others:
+        pl.semaphore_signal(
+            barrier, inc=1, device_id={"tensor": c, "shard": t}, device_id_type=MESH
+        )
+    pl.semaphore_wait(barrier, 7)
+
+    def remote(src, dst, sems, i, device):
+        return pltpu.make_async_remote_copy(
+            src_ref=src,
+            dst_ref=dst,
+            send_sem=sems.at[0, i],
+            recv_sem=sems.at[1, i],
+            device_id=device,
+            device_id_type=MESH,
+        )
+
+    def rows_at(start):
+        return pl.ds(pl.multiple_of(start, 8), piece)
+
+    sibling = {"tensor": 1 - core}
+    order = [lax.rem(s + k, 4) for k in (1, 2, 3, 0)]
+    pair = []
+    for i, t in enumerate(order):
+        rows = rows_at(t * piece)
+        copy = remote(
+            x_ref.at[rows_at((1 - core) * half + t * piece)], abuf.at[rows], a_sem, i, sibling
+        )
+        copy.start()
+        pair.append(copy)
+    me = core * 4 + s
+    squares = []
+    for i, (c, t) in enumerate(others):
+        copy = remote(sq_ref, sqbuf.at[me], s_sem, i, {"tensor": c, "shard": t})
+        copy.start()
+        squares.append(copy)
+    spread = []
+    for i, t in enumerate(order):
+        rows = rows_at(t * piece)
+        pair[i].wait_recv()
+        hbuf[rows, :] = x_ref[rows_at(core * half + t * piece), :] + abuf[rows, :]
+        if i < 3:
+            copy = remote(hbuf.at[rows], bbuf.at[i], b_sem, i, {"shard": t})
+            copy.start()
+            spread.append(copy)
+    mine = rows_at(core * half + s * piece)
+    for copy in spread:
+        copy.wait_recv()
+    out_ref[mine, :] = (hbuf[rows_at(s * piece), :] + bbuf[0]) + (bbuf[1] + bbuf[2])
+    gather = []
+    for i in range(3):
+        copy = remote(out_ref.at[mine], out_ref.at[mine], c_sem, i, {"shard": order[i]})
+        copy.start()
+        gather.append(copy)
+    across = [remote(out_ref.at[mine], out_ref.at[mine], d_sem, 3, sibling)]
+    across[0].start()
+    for i in range(3):
+        gather[i].wait_recv()
+        rows = rows_at(core * half + lax.rem(s + 3 - i, 4) * piece)
+        copy = remote(out_ref.at[rows], out_ref.at[rows], d_sem, i, sibling)
+        copy.start()
+        across.append(copy)
+    for copy in squares:
+        copy.wait()
+    sqbuf[pl.ds(me, 1)] = sq_ref[...][None]
+    sq_out[...] = jnp.sum(sqbuf[...], axis=0)
+    for copy in across:
+        copy.wait()
+    for copy in pair + spread + gather:
+        copy.wait_send()
+
+
+def plane_sum(partial, squares):
+    rows, rank = partial.shape
+    piece = rows // 8
+    dma = pltpu.SemaphoreType.DMA
+    return pl.pallas_call(
+        plane_sum_kernel,
+        out_shape=(
+            jax.ShapeDtypeStruct(partial.shape, jnp.float32),
+            jax.ShapeDtypeStruct(squares.shape, jnp.float32),
+        ),
+        in_specs=[VMEM, VMEM],
+        out_specs=(VMEM, VMEM),
+        scratch_shapes=[
+            pltpu.VMEM((rows // 2, rank), jnp.float32),
+            pltpu.VMEM((rows // 2, rank), jnp.float32),
+            pltpu.VMEM((3, piece, rank), jnp.float32),
+            pltpu.VMEM((8,) + squares.shape, jnp.float32),
+            dma((2, 4)),
+            dma((2, 3)),
+            dma((2, 3)),
+            dma((2, 4)),
+            dma((2, 7)),
+        ],
+        compiler_params=pltpu.CompilerParams(collective_id=2, has_side_effects=True),
+    )(partial, squares)
+
+
+def gather_kernel(ch, rate, delta_ref, w_ref, out_ref, rbuf, own_sem, fwd_sem, recv_sem):
+    s = lax.axis_index("shard")
+    y, x = s // 2, lax.rem(s, 2)
+    source = (y * 2 + (1 - x), (1 - y) * 2 + x, (1 - y) * 2 + (1 - x))
+    barrier = pltpu.get_barrier_semaphore()
+    for r in range(2):
+        pl.semaphore_signal(barrier, inc=1, device_id={"shard": source[r]}, device_id_type=MESH)
+    pl.semaphore_wait(barrier, 2)
+    mats, rows, cols = delta_ref.shape
+    per = rows // ch
+    nch = mats * per
+
+    def place(ref, j):
+        return ref.at[j // per, pl.ds(pl.multiple_of(lax.rem(j, per) * ch, 8), ch)]
+
+    def own(r, j):
+        return pltpu.make_async_remote_copy(
+            src_ref=place(delta_ref, j),
+            dst_ref=place(rbuf.at[r], j),
+            send_sem=own_sem.at[r, j],
+            recv_sem=recv_sem.at[r, j],
+            device_id={"shard": source[r]},
+            device_id_type=MESH,
+        )
+
+    def forward(r, j):
+        return pltpu.make_async_remote_copy(
+            src_ref=place(rbuf.at[1 - r], j),
+            dst_ref=place(rbuf.at[2], j),
+            send_sem=fwd_sem.at[j],
+            recv_sem=recv_sem.at[2, j],
+            device_id={"shard": source[r]},
+            device_id_type=MESH,
+        )
+
+    def start(j, carry):
+        for r in range(2):
+            own(r, j).start()
+        return carry
+
+    lax.fori_loop(0, nch, start, 0)
+
+    def write(j, src, chunk):
+        m = j // per
+        at = pl.ds(pl.multiple_of(lax.rem(j, per) * ch, 8), ch)
+        for t in range(4):
+
+            @pl.when(src == t)
+            def _():
+                lanes = slice(t * cols, (t + 1) * cols)
+                out_ref[m, at, lanes] = w_ref[m, at, lanes] - rate * chunk[...]
+
+    def near(j, carry):
+        for r in range(2):
+            own(r, j).wait_recv()
+        for r in range(2):
+
+            @pl.when(lax.rem(j, 2) == r)
+            def _():
+                forward(r, j).start()
+
+        write(j, s, place(delta_ref, j))
+        for r in range(2):
+            write(j, source[r], place(rbuf.at[r], j))
+        return carry
+
+    lax.fori_loop(0, nch, near, 0)
+
+    def far(j, carry):
+        forward(0, j).wait()
+        write(j, source[2], place(rbuf.at[2], j))
+        for r in range(2):
+            own(r, j).wait_send()
+        return carry
+
+    lax.fori_loop(0, nch, far, 0)
+
+
+def gather_update(delta, weights, rate):
+    mats, rows, cols = delta.shape
+    ch = chunk_rows(rows, 56)
+    nch = mats * (rows // ch)
+    dma = pltpu.SemaphoreType.DMA
+    return pl.pallas_call(
+        functools.partial(gather_kernel, ch, rate),
+        out_shape=jax.ShapeDtypeStruct(weights.shape, jnp.float32),
+        in_specs=[VMEM, VMEM],
+        out_specs=VMEM,
+        scratch_shapes=[
+            pltpu.VMEM((3, mats, rows, cols), jnp.float32),
+            dma((2, nch)),
+            dma((nch,)),
+            dma((3, nch)),
+        ],
+        compiler_params=pltpu.CompilerParams(
+            collective_id=3, has_side_effects=True, vmem_limit_bytes=40 * 2**20
+        ),
+    )(delta, weights)
 
 
 def per_device(
@@ -242,19 +483,20 @@
     gain_second,
 ):
     z = lax.axis_index("dp")
-    ff = first_moment.shape[2] * lax.axis_size(("tensor", "shard"))
-    mine, gain_total = line_sum(dp, grads[0], gain_grad)
+    shards = lax.axis_size("shard")
+    ff = first_moment.shape[2] * lax.axis_size("tensor") * shards
+    mine, gain_total = line_sum(dp, jnp.swapaxes(grads[0], 1, 2), gain_grad)
     gain_total = gain_total[0]
     basis = lax.dynamic_index_in_dim(bases, jnp.where(z * 2 >= dp, 1, 0), 0, keepdims=False)
     rows, rank = basis.shape
-    local_squares = jnp.sum(mine * mine)
-    carried = dot(mine, basis, ((0,), (0,)))
-    partial = dot(mine, carried, ((1,), (0,)))
-    packed = jnp.concatenate(
-        [partial, jnp.full((8, rank), local_squares, jnp.float32)], axis=0
-    )
-    packed = lax.psum(packed, ("tensor", "shard"))
-    sketch, squares = packed[:rows], packed[rows:, :128]
+    squares = jnp.full((8, 128), jnp.sum(mine * mine), jnp.float32)
+    carried = dot(mine, basis, ((1,), (0,)))
+    partial = dot(mine, carried, ((0,), (0,)))
+    direct = shards == 4 and lax.axis_size("tensor") == 2 and rows % 64 == 0
+    if direct:
+        sketch, squares = plane_sum(partial, squares)
+    else:
+        sketch, squares = lax.psum((partial, squares), ("tensor", "shard"))
     iterate = sketch / (jnp.sqrt(jnp.sum(sketch * sketch)) + norm_eps)
     gram = dot(iterate, iterate, ((0,), (0,)))
     eye = jnp.eye(rank, dtype=jnp.float32)
@@ -265,30 +507,39 @@
         if turn < NS_STEPS - 1:
             gram = dot(dot(factor, gram, ((1,), (0,))), factor, ((1,), (0,)))
     new_basis = dot(iterate, product, ((1,), (0,)))
-    projected = dot(new_basis, mine, ((0,), (0,)))
-    projected, squares, new_bases = line_spread(dp, (projected, squares, new_basis), (8, 1, 7))
+    projected = dot(mine, new_basis, ((1,), (0,)))
+    projected, squares, new_bases = line_spread(
+        dp,
+        (projected, squares, new_basis),
+        (chunk_rows(projected.shape[0], 32), 8, chunk_rows(rows // 2, 64)),
+    )
 
     total_squares = squares[0, 0, 0] + squares[1, 0, 0] + jnp.sum(gain_total * gain_total)
     clip_factor = jnp.minimum(1.0, math.sqrt(MATS * ff) / (jnp.sqrt(total_squares) + norm_eps))
     bias_one = 1.0 - beta_one**adam_step
     bias_two = 1.0 - beta_two**adam_step
     projected_gradient = clip_factor * projected
-    new_first = beta_one * first_moment + (1.0 - beta_one) * projected_gradient
+    new_first = beta_one * jnp.swapaxes(first_moment, 1, 2) + (1.0 - beta_one) * projected_gradient
     new_second = (
-        beta_two * second_moment + (1.0 - beta_two) * projected_gradient * projected_gradient
+        beta_two * jnp.swapaxes(second_moment, 1, 2)
+        + (1.0 - beta_two) * projected_gradient * projected_gradient
     )
     direction = new_first / bias_one / (jnp.sqrt(new_second / bias_two) + adam_eps)
+    new_first, new_second = jnp.swapaxes(new_first, 1, 2), jnp.swapaxes(new_second, 1, 2)
     row_count = weights.shape[1]
     slab = lax.dynamic_slice_in_dim(new_bases, z * row_count, row_count, 1)
     delta = lax.dot_general(
         slab,
         direction,
-        (((2,), (1,)), ((0,), (0,))),
+        (((2,), (2,)), ((0,), (0,))),
         precision=lax.Precision.HIGH,
         preferred_element_type=jnp.float32,
     )
-    delta = lax.all_gather(delta, "shard", axis=2, tiled=True)
-    new_weights = weights - learn_rate * galore_scale * delta
+    if direct:
+        new_weights = gather_update(delta, weights, learn_rate * galore_scale)
+    else:
+        delta = lax.all_gather(delta, "shard", axis=2, tiled=True)
+        new_weights = weights - learn_rate * galore_scale * delta
     clipped_gain = clip_factor * gain_total
     gain_first_new = beta_one * gain_first + (1.0 - beta_one) * clipped_gain
     gain_second_new = beta_two * gain_second + (1.0 - beta_two) * clipped_gain * clipped_gain

time: 305 us -> 212 us (0.70)
  waiting for transfers between devices: 95 us -> 0 us
  Pallas kernels: 115 us -> 172 us
  local copies, waits for them, and re-layouts: 45.6 us -> 12.9 us
  between operations: 17.1 us -> 3.71 us
  other arithmetic: 15.6 us -> 6.23 us
    pallas_call x0 -> x2, Pallas kernels: none -> 61.6 us  [the longest x1 40.5 us: gather_update(): pl.pallas_call(functools.partial(gather_kernel, ch, rate), out_shape=jax....]
    psum x1 -> x0, waiting for transfers between devices: 51.4 us -> none  [per_device(): packed = lax.psum(packed, ('tensor', 'shard'))]
    all_gather x1 -> x0, waiting for transfers between devices: 43.5 us -> none  [per_device(): delta = lax.all_gather(delta, 'shard', axis=2, tiled=True)]
    unnamed x38 -> x36, local copies, waits for them, and re-layouts: 41.9 us -> 11.1 us
    sub x1 -> x0, other arithmetic: 8.99 us -> none  [per_device(): new_weights = weights - learn_rate * galore_scale * delta]
    pallas_call x1, Pallas kernels: 66.6 us -> 61.5 us  [line_sum(): pl.pallas_call(functools.partial(line_sum_kernel, dp, ch), out_shape=(jax...]
  transfers between devices with their start and end apart: 2 -> 0, of which waited for: 2 -> 0; matrix products, arithmetic and copies ran while one was open for 6% -> 0% of each run, Pallas kernels for 0% -> 0%
where the time goes in v2:
time: 212 us
  Pallas kernels  172 us (81%)
  matrix products  16.9 us (8%)
  local copies, waits for them, and re-layouts  12.9 us (6%)
  other arithmetic  6.23 us (3%)
  between operations  3.71 us (2%)
    pallas_call x1, Pallas kernels, line_sum(): pl.pallas_call(functools.partial(line_sum_kernel, dp, ch), out_shape=(jax...  61.5 us
    pallas_call x1, Pallas kernels, line_spread(): pl.pallas_call(functools.partial(line_spread_kernel, dp, parts), out_shap...  49 us
    pallas_call x1, Pallas kernels, gather_update(): pl.pallas_call(functools.partial(gather_kernel, ch, rate), out_shape=jax....  40.5 us
    pallas_call x1, Pallas kernels, plane_sum(): pl.pallas_call(plane_sum_kernel, out_shape=(jax.ShapeDtypeStruct(partial....  21.1 us
    dot_general x17, matrix products, dot(): lax.dot_general(left, right, (dims, ((), ())), precision=precision, prefe...  13.4 us
    unnamed x36, local copies, waits for them, and re-layouts  11.1 us

profile of v2, /device:TPU:0, one launch (start us, length us, event | category | flops | bytes accessed | tf_op | source)
XLA Modules:
  0.0 211.8 jit_solution(13909379503186426269)
XLA Ops:
  0.7 2.4 %copy-done.4 = f32[1,2,896,608]{2,3,1,0:T(8,128)S(1)} copy-done((f32[1,2,896,608]{2,3,1,0:T(8,128)S(1)}, f32[1,2,896,608]{2,3,1,0:T(8,128)}, u32[]{:S(2)}) %copy-start.4) | copy-done | bytes 4358168
  3.0 0.7 copy-done.8
  3.7 61.5 %shard_map.144 = (f32[608,896]{1,0:T(8,128)S(1)}, f32[1,896]{1,0:T(1,128)S(1)}) custom-call(f32[2,608,896]{2,1,0:T(8,128)S(1)} %bitcast.45, f32[1,896]{1,0:T(1,128)S(1)} %copy-done.8), custom_call_target="tpu_custom_call" | custom-call | tf_op jit(solution)/shard_map/pallas_call | solution.py:137
  65.2 1.3 copy-done.1
  66.6 2.9 %fusion.8 = f32[608,256]{1,0:T(8,128)S(1)} fusion(f32[608,896]{1,0:T(8,128)} %copy-done.1, f32[2,896,256]{2,1,0:T(8,128)S(1)} %copy-done, s32[]{:T(128)S(6)} %select_n.9), kind=kOutput, calls=%fused_computation.12 | convolution fusion | flops 836763648 | bytes 3719172 | tf_op jit(solution)/shard_map/dot_general | solution.py:28
  69.5 3.0 %fusion.108.x_ref = f32[896,256]{1,0:T(8,128)} fusion(f32[608,896]{1,0:T(8,128)S(1)} %copy-done.2, f32[608,256]{1,0:T(8,128)S(1)} %fusion.8), kind=kOutput, calls=%fused_computation.122 | convolution fusion | flops 836763648 | bytes 3719168 | tf_op jit(solution)/shard_map/dot_general | solution.py:28
  72.5 1.2 multiply_reduce_fusion
  73.6 1.2 broadcast_in_dim.3.sq_ref
  74.9 21.1 %shard_map.145 = (f32[896,256]{1,0:T(8,128)}, f32[8,128]{1,0:T(8,128)}) custom-call(f32[896,256]{1,0:T(8,128)} %fusion.108.x_ref, f32[8,128]{1,0:T(8,128)} %broadcast_in_dim.3.sq_ref), custom_call_target="tpu_custom_call" | custom-call | tf_op jit(solution)/shard_map/pallas_call | solution.py:350
  95.9 2.0 multiply_reduce_fusion.1
  98.7 2.4 %fusion.16 = f32[256,256]{1,0:T(8,128)S(1)} fusion(f32[896,256]{1,0:T(8,128)} %get-tuple-element.15, f32[]{:T(128)S(6)} %add.44), kind=kOutput, calls=%fused_computation.26 | convolution fusion | flops 352550912 | bytes 1179652 | tf_op jit(solution)/shard_map/dot_general | solution.py:28
  101.3 0.3 fusion.21
  101.6 0.3 fusion.20
  102.2 0.3 fusion.23
  102.5 0.3 fusion.27
  103.1 0.3 fusion.25
  103.4 0.3 fusion.19
  104.6 0.3 copy-done.11
  104.9 0.5 fusion.15.refs_2_
  105.4 1.1 copy-done.3
  106.5 1.2 fusion.110.refs_0_
  107.7 49.0 %shard_map.146 = (f32[2,608,256]{2,1,0:T(8,128)S(1)}, f32[2,8,128]{2,1,0:T(8,128)S(1)}, f32[2,896,256]{2,1,0:T(8,128)S(1)}) custom-call(f32[608,256]{1,0:T(8,128)S(1)} %fusion.110.refs_0_, f32[8,128]{1,0:T(8,128)S(1)} %copy-done.7, f32[896,256]{1,0:T(8,128)S(1)} %fusion.15.refs_2_), custom_call_target="tpu_custom_call" | custom-call | tf_op jit(solution)/shard_map/pallas_call | solution.py:255
  156.7 1.2 copy-done.5
  157.9 0.5 fusion.107
  159.7 0.6 multiply_reduce_fusion.3
  161.1 3.6 %fusion.1.delta_ref = f32[2,224,608]{2,1,0:T(8,128)S(1)} fusion(f32[2,896,256]{2,1,0:T(8,128)} %copy-done.5, s32[]{:T(128)S(6)} %select_n.10, f32[2,256,608]{1,2,0:T(8,128)} %param.12, f32[2,608,256]{2,1,0:T(8,128)S(1)} %get-tuple-element.20, f32[]{:T(128)S(6)} %min_shard_map.3, f32[2,256,608]{1,2,0:T(8,128)} %param.13), kind=kOutput, calls=%fused_computation.4 | convolution fusion | flops 422117376 | bytes 5283848 | tf_op jit(solution)/shard_map/dot_general | solution.py:531
  164.7 40.5 %shard_map.147 = f32[2,224,2432]{2,1,0:T(8,128)S(1)} custom-call(f32[2,224,608]{2,1,0:T(8,128)S(1)} %fusion.1.delta_ref, f32[2,224,2432]{2,1,0:T(8,128)S(1)} %bitcast.44), custom_call_target="tpu_custom_call" | custom-call | tf_op jit(solution)/shard_map/pallas_call | solution.py:456
  205.3 1.8 fusion.28
  207.2 0.6 divide_subtract_fusion
  207.8 2.1 copy.18
  209.9 0.7 copy-done.6
  210.6 1.2 copy.19
  (35 shorter events, 1.8 us)
Async XLA Ops:
  0.6 65.9 %copy-start = (f32[2,896,256]{2,1,0:T(8,128)S(1)}, f32[2,896,256]{2,1,0:T(8,128)}, u32[]{:S(2)}) copy-start(f32[2,896,256]{2,1,0:T(8,128)} %param.11) | copy-start | bytes 5505028
  0.6 2.4 %copy-start.4 = (f32[1,2,896,608]{2,3,1,0:T(8,128)S(1)}, f32[1,2,896,608]{2,3,1,0:T(8,128)}, u32[]{:S(2)}) copy-start(f32[1,2,896,608]{2,3,1,0:T(8,128)} %param.10) | copy-start | bytes 13074436
  3.0 0.7 copy-start.8
  65.2 1.3 copy-start.1
  66.6 2.9 %copy-start.2 = (f32[608,896]{1,0:T(8,128)S(1)}, f32[608,896]{1,0:T(8,128)}, u32[]{:S(2)}) copy-start(f32[608,896]{1,0:T(8,128)} %copy-done.1) | copy-start | bytes 6537220
  103.7 1.2 copy-start.11
  104.9 1.6 copy-start.3
  106.5 1.2 copy-start.7
  107.7 57.0 %slice-start = ((s8[4358144]{0:T(1024)(128)(4,1)}), s8[163840]{0:T(1024)(128)(4,1)S(1)}, s32[]{:S(2)}) async-start(s8[4358144]{0:T(1024)(128)(4,1)} %bitcast.43), calls=%async_computation | async-start | bytes 327680
  156.7 1.2 copy-start.5
  161.1 3.6 %slice-start.1 = ((s8[4358144]{0:T(1024)(128)(4,1)}), s8[4194304]{0:T(1024)(128)(4,1)S(1)}, s32[]{:S(2)}) async-start(s8[4358144]{0:T(1024)(128)(4,1)} %bitcast.43), calls=%async_computation.1 | async-start | bytes 8388608
  164.7 40.6 %copy-start.9 = (f32[2,256,608]{1,2,0:T(8,128)S(1)}, f32[2,256,608]{1,2,0:T(8,128)}, u32[]{:S(2)}) copy-start(f32[2,256,608]{1,2,0:T(8,128)} %param.12) | copy-start | bytes 3735556
  164.7 40.6 %copy-start.10 = (f32[2,256,608]{1,2,0:T(8,128)S(1)}, f32[2,256,608]{1,2,0:T(8,128)}, u32[]{:S(2)}) copy-start(f32[2,256,608]{1,2,0:T(8,128)} %param.13) | copy-start | bytes 3735556
  205.3 1.9 copy-start.12
  205.3 1.9 copy-start.13
  205.3 1.9 copy-start.14
  207.8 2.8 %copy-start.6 = (f32[2,896,256]{2,1,0:T(8,128)S(1)}, f32[2,896,256]{2,1,0:T(8,128)}, u32[]{:S(2)}) copy-start(f32[2,896,256]{2,1,0:T(8,128)} %copy-done.5) | copy-start | bytes 5505028

commit v3 on v2

--- a/solution.py
+++ b/solution.py
@@ -21,7 +21,8 @@
 
 MESH = pl.DeviceIdType.MESH
 VMEM = pl.BlockSpec(memory_space=pltpu.VMEM)
-SKEW = 2
+SUM_SKEW = 4
+SPREAD_SKEW = 8
 
 
 def dot(left, right, dims, precision=lax.Precision.HIGH):
@@ -70,7 +71,7 @@
 
     def step(i, carry):
         for m in range(MATS):
-            c = i - SKEW * hops[m]
+            c = i - SUM_SKEW * hops[m]
             live = jnp.logical_and(c >= 0, c < nch)
             rows = pl.ds(pl.multiple_of(c * ch, 8), ch)
 
@@ -106,7 +107,7 @@
         copy.start()
         gcopies.append(copy)
 
-    lax.fori_loop(0, nch + SKEW * (dp - 1), step, 0)
+    lax.fori_loop(0, nch + SUM_SKEW * (dp - 1), step, 0)
 
     for copy in gcopies:
         copy.wait()
@@ -131,7 +132,7 @@
 
 def line_sum(dp, grads, gain_grad):
     mats, rows, cols = grads.shape
-    ch = chunk_rows(rows, 32)
+    ch = chunk_rows(rows, 16)
     nch = rows // ch
     dma = pltpu.SemaphoreType.DMA
     return pl.pallas_call(
@@ -215,10 +216,10 @@
             for a in range(n):
                 pltpu.make_async_copy(ins[a], outs[a].at[m], keep.at[a]).start()
 
-    for i in range(len(plan) + SKEW * (dp - 1)):
+    for i in range(len(plan) + SPREAD_SKEW * (dp - 1)):
         for m in range(MATS):
             for h in range(1, dp):
-                k = i - SKEW * h
+                k = i - SPREAD_SKEW * h
                 if 0 <= k < len(plan):
 
                     @pl.when(hops[m] == h)

time: 212 us -> 207 us (0.976)
  Pallas kernels: 172 us -> 166 us
    pallas_call x1, Pallas kernels: 49 us -> 42.7 us  [line_spread(): pl.pallas_call(functools.partial(line_spread_kernel, dp, parts), out_shap...]
where the time goes in v3:
time: 207 us; the launch traced here: 206 us
  Pallas kernels  166 us (80%)
  matrix products  16.9 us (8%)
  local copies, waits for them, and re-layouts  12.9 us (6%)
  other arithmetic  6.23 us (3%)
  between operations  3.71 us (2%)
    pallas_call x1, Pallas kernels, line_sum(): pl.pallas_call(functools.partial(line_sum_kernel, dp, ch), out_shape=(jax...  62.1 us
    pallas_call x1, Pallas kernels, line_spread(): pl.pallas_call(functools.partial(line_spread_kernel, dp, parts), out_shap...  42.7 us
    pallas_call x1, Pallas kernels, gather_update(): pl.pallas_call(functools.partial(gather_kernel, ch, rate), out_shape=jax....  40.5 us
    pallas_call x1, Pallas kernels, plane_sum(): pl.pallas_call(plane_sum_kernel, out_shape=(jax.ShapeDtypeStruct(partial....  21.1 us
    dot_general x17, matrix products, dot(): lax.dot_general(left, right, (dims, ((), ())), precision=precision, prefe...  13.4 us
    unnamed x36, local copies, waits for them, and re-layouts  11.1 us

profile of v3, /device:TPU:0, one launch (start us, length us, event | category | flops | bytes accessed | tf_op | source)
XLA Modules:
  0.0 206.2 jit_solution(11774527804952483337)
XLA Ops:
  0.7 2.4 %copy-done.4 = f32[1,2,896,608]{2,3,1,0:T(8,128)S(1)} copy-done((f32[1,2,896,608]{2,3,1,0:T(8,128)S(1)}, f32[1,2,896,608]{2,3,1,0:T(8,128)}, u32[]{:S(2)}) %copy-start.4) | copy-done | bytes 4358168
  3.0 0.7 copy-done.8
  3.7 62.1 %shard_map.144 = (f32[608,896]{1,0:T(8,128)S(1)}, f32[1,896]{1,0:T(1,128)S(1)}) custom-call(f32[2,608,896]{2,1,0:T(8,128)S(1)} %bitcast.45, f32[1,896]{1,0:T(1,128)S(1)} %copy-done.8), custom_call_target="tpu_custom_call" | custom-call | tf_op jit(solution)/shard_map/pallas_call | solution.py:138
  65.8 1.3 copy-done.1
  67.2 2.9 %fusion.8 = f32[608,256]{1,0:T(8,128)S(1)} fusion(f32[608,896]{1,0:T(8,128)} %copy-done.1, f32[2,896,256]{2,1,0:T(8,128)S(1)} %copy-done, s32[]{:T(128)S(6)} %select_n.9), kind=kOutput, calls=%fused_computation.12 | convolution fusion | flops 836763648 | bytes 3719172 | tf_op jit(solution)/shard_map/dot_general | solution.py:29
  70.1 3.0 %fusion.108.x_ref = f32[896,256]{1,0:T(8,128)} fusion(f32[608,896]{1,0:T(8,128)S(1)} %copy-done.2, f32[608,256]{1,0:T(8,128)S(1)} %fusion.8), kind=kOutput, calls=%fused_computation.122 | convolution fusion | flops 836763648 | bytes 3719168 | tf_op jit(solution)/shard_map/dot_general | solution.py:29
  73.1 1.2 multiply_reduce_fusion
  74.2 1.2 broadcast_in_dim.3.sq_ref
  75.5 21.1 %shard_map.145 = (f32[896,256]{1,0:T(8,128)}, f32[8,128]{1,0:T(8,128)}) custom-call(f32[896,256]{1,0:T(8,128)} %fusion.108.x_ref, f32[8,128]{1,0:T(8,128)} %broadcast_in_dim.3.sq_ref), custom_call_target="tpu_custom_call" | custom-call | tf_op jit(solution)/shard_map/pallas_call | solution.py:351
  96.5 2.0 multiply_reduce_fusion.1
  99.3 2.4 %fusion.16 = f32[256,256]{1,0:T(8,128)S(1)} fusion(f32[896,256]{1,0:T(8,128)} %get-tuple-element.15, f32[]{:T(128)S(6)} %add.44), kind=kOutput, calls=%fused_computation.26 | convolution fusion | flops 352550912 | bytes 1179652 | tf_op jit(solution)/shard_map/dot_general | solution.py:29
  101.9 0.3 fusion.21
  102.2 0.3 fusion.20
  102.8 0.3 fusion.23
  103.1 0.3 fusion.27
  103.7 0.3 fusion.25
  104.0 0.3 fusion.19
  105.2 0.3 copy-done.11
  105.5 0.5 fusion.15.refs_2_
  106.0 1.1 copy-done.3
  107.1 1.2 fusion.110.refs_0_
  108.3 42.7 %shard_map.146 = (f32[2,608,256]{2,1,0:T(8,128)S(1)}, f32[2,8,128]{2,1,0:T(8,128)S(1)}, f32[2,896,256]{2,1,0:T(8,128)S(1)}) custom-call(f32[608,256]{1,0:T(8,128)S(1)} %fusion.110.refs_0_, f32[8,128]{1,0:T(8,128)S(1)} %copy-done.7, f32[896,256]{1,0:T(8,128)S(1)} %fusion.15.refs_2_), custom_call_target="tpu_custom_call" | custom-call | tf_op jit(solution)/shard_map/pallas_call | solution.py:256
  151.0 1.2 copy-done.5
  152.2 0.5 fusion.107
  154.1 0.6 multiply_reduce_fusion.3
  155.4 3.6 %fusion.1.delta_ref = f32[2,224,608]{2,1,0:T(8,128)S(1)} fusion(f32[2,896,256]{2,1,0:T(8,128)} %copy-done.5, s32[]{:T(128)S(6)} %select_n.10, f32[2,256,608]{1,2,0:T(8,128)} %param.12, f32[2,608,256]{2,1,0:T(8,128)S(1)} %get-tuple-element.20, f32[]{:T(128)S(6)} %min_shard_map.3, f32[2,256,608]{1,2,0:T(8,128)} %param.13), kind=kOutput, calls=%fused_computation.4 | convolution fusion | flops 422117376 | bytes 5283848 | tf_op jit(solution)/shard_map/dot_general | solution.py:532
  159.0 40.5 %shard_map.147 = f32[2,224,2432]{2,1,0:T(8,128)S(1)} custom-call(f32[2,224,608]{2,1,0:T(8,128)S(1)} %fusion.1.delta_ref, f32[2,224,2432]{2,1,0:T(8,128)S(1)} %bitcast.44), custom_call_target="tpu_custom_call" | custom-call | tf_op jit(solution)/shard_map/pallas_call | solution.py:457
  199.7 1.8 fusion.28
  201.5 0.6 divide_subtract_fusion
  202.1 2.1 %copy.18 = f32[2,224,2432]{2,1,0:T(8,128)} copy(f32[2,224,2432]{2,1,0:T(8,128)S(1)} %shard_map.147) | data formatting | bytes 8716288
  204.2 0.7 copy-done.6
  205.0 1.2 copy.19
  (35 shorter events, 1.8 us)
Async XLA Ops:
  0.6 66.5 %copy-start = (f32[2,896,256]{2,1,0:T(8,128)S(1)}, f32[2,896,256]{2,1,0:T(8,128)}, u32[]{:S(2)}) copy-start(f32[2,896,256]{2,1,0:T(8,128)} %param.11) | copy-start | bytes 5505028
  0.6 2.4 %copy-start.4 = (f32[1,2,896,608]{2,3,1,0:T(8,128)S(1)}, f32[1,2,896,608]{2,3,1,0:T(8,128)}, u32[]{:S(2)}) copy-start(f32[1,2,896,608]{2,3,1,0:T(8,128)} %param.10) | copy-start | bytes 13074436
  3.0 0.7 copy-start.8
  65.8 1.3 copy-start.1
  67.2 2.9 %copy-start.2 = (f32[608,896]{1,0:T(8,128)S(1)}, f32[608,896]{1,0:T(8,128)}, u32[]{:S(2)}) copy-start(f32[608,896]{1,0:T(8,128)} %copy-done.1) | copy-start | bytes 6537220
  104.3 1.2 copy-start.11
  105.5 1.6 copy-start.3
  107.1 1.2 copy-start.7
  108.3 50.7 %slice-start = ((s8[4358144]{0:T(1024)(128)(4,1)}), s8[163840]{0:T(1024)(128)(4,1)S(1)}, s32[]{:S(2)}) async-start(s8[4358144]{0:T(1024)(128)(4,1)} %bitcast.43), calls=%async_computation | async-start | bytes 327680
  151.0 1.2 copy-start.5
  155.4 3.6 %slice-start.1 = ((s8[4358144]{0:T(1024)(128)(4,1)}), s8[4194304]{0:T(1024)(128)(4,1)S(1)}, s32[]{:S(2)}) async-start(s8[4358144]{0:T(1024)(128)(4,1)} %bitcast.43), calls=%async_computation.1 | async-start | bytes 8388608
  159.0 40.6 %copy-start.9 = (f32[2,256,608]{1,2,0:T(8,128)S(1)}, f32[2,256,608]{1,2,0:T(8,128)}, u32[]{:S(2)}) copy-start(f32[2,256,608]{1,2,0:T(8,128)} %param.12) | copy-start | bytes 3735556
  159.0 40.6 %copy-start.10 = (f32[2,256,608]{1,2,0:T(8,128)S(1)}, f32[2,256,608]{1,2,0:T(8,128)}, u32[]{:S(2)}) copy-start(f32[2,256,608]{1,2,0:T(8,128)} %param.13) | copy-start | bytes 3735556
  199.6 1.9 copy-start.12
  199.6 1.9 copy-start.13
  199.6 1.9 copy-start.14
  202.1 2.8 %copy-start.6 = (f32[2,896,256]{2,1,0:T(8,128)S(1)}, f32[2,896,256]{2,1,0:T(8,128)}, u32[]{:S(2)}) copy-start(f32[2,896,256]{2,1,0:T(8,128)} %copy-done.5) | copy-start | bytes 5505028

commit v4 on v3

--- a/solution.py
+++ b/solution.py
@@ -49,7 +49,7 @@
 
 
 def line_sum_kernel(
-    dp, ch, g_ref, gain_ref, out_ref, gain_out, rbuf, gbuf, send, recv, gsend, grecv
+    dp, ch, g_ref, gain_ref, out_ref, gain_out, sq_out, rbuf, gbuf, acc, send, recv, gsend, grecv
 ):
     z = lax.axis_index("dp")
     nch = g_ref.shape[1] // ch
@@ -90,10 +90,14 @@
 
             @pl.when(jnp.logical_and(live, hops[m] == dp - 1))
             def _():
-                out_ref[rows, :] = rbuf[m, rows, :] + g_ref[m, rows, :]
+                total = rbuf[m, rows, :] + g_ref[m, rows, :]
+                out_ref[rows, :] = total
+                for r in range(0, ch, 8):
+                    acc[...] += total[r : r + 8] * total[r : r + 8]
 
         return carry
 
+    acc[...] = jnp.zeros_like(acc)
     gcopies = []
     for k in range(1, dp):
         copy = pltpu.make_async_remote_copy(
@@ -113,6 +117,8 @@
         copy.wait()
     gbuf[pl.ds(z, 1)] = gain_ref[...][None]
     gain_out[...] = jnp.sum(gbuf[...], axis=0)
+    squares = jnp.sum(jnp.sum(acc[...], axis=1, keepdims=True), axis=0, keepdims=True)
+    sq_out[...] = jnp.broadcast_to(squares, sq_out.shape)
 
     @pl.when(jnp.logical_and(z > 0, z < dp - 1))
     def _():
@@ -140,12 +146,14 @@
         out_shape=(
             jax.ShapeDtypeStruct((rows, cols), jnp.float32),
             jax.ShapeDtypeStruct(gain_grad.shape, jnp.float32),
+            jax.ShapeDtypeStruct((8, 128), jnp.float32),
         ),
         in_specs=[VMEM, VMEM],
-        out_specs=(VMEM, VMEM),
+        out_specs=(VMEM, VMEM, VMEM),
         scratch_shapes=[
             pltpu.VMEM((mats, rows, cols), jnp.float32),
             pltpu.VMEM((dp,) + gain_grad.shape, jnp.float32),
+            pltpu.VMEM((8, cols), jnp.float32),
             dma((mats, nch)),
             dma((mats, nch)),
             dma((dp,)),
@@ -451,7 +459,7 @@
 
 def gather_update(delta, weights, rate):
     mats, rows, cols = delta.shape
-    ch = chunk_rows(rows, 56)
+    ch = chunk_rows(rows, 32)
     nch = mats * (rows // ch)
     dma = pltpu.SemaphoreType.DMA
     return pl.pallas_call(
@@ -486,11 +494,10 @@
     z = lax.axis_index("dp")
     shards = lax.axis_size("shard")
     ff = first_moment.shape[2] * lax.axis_size("tensor") * shards
-    mine, gain_total = line_sum(dp, jnp.swapaxes(grads[0], 1, 2), gain_grad)
+    mine, gain_total, squares = line_sum(dp, jnp.swapaxes(grads[0], 1, 2), gain_grad)
     gain_total = gain_total[0]
     basis = lax.dynamic_index_in_dim(bases, jnp.where(z * 2 >= dp, 1, 0), 0, keepdims=False)
     rows, rank = basis.shape
-    squares = jnp.full((8, 128), jnp.sum(mine * mine), jnp.float32)
     carried = dot(mine, basis, ((1,), (0,)))
     partial = dot(mine, carried, ((0,), (0,)))
     direct = shards == 4 and lax.axis_size("tensor") == 2 and rows % 64 == 0

time: 207 us -> 205 us (level)
    unnamed x36 -> x38, local copies, waits for them, and re-layouts: 11.1 us -> 11.7 us
where the time goes in v4:
time: 205 us
  Pallas kernels  167 us (81%)
  matrix products  16.9 us (8%)
  local copies, waits for them, and re-layouts  12.2 us (6%)
  other arithmetic  5.07 us (2%)
  between operations  3.71 us (2%)
    pallas_call x1, Pallas kernels, line_sum(): pl.pallas_call(functools.partial(line_sum_kernel, dp, ch), out_shape=(jax...  62.2 us
    pallas_call x1, Pallas kernels, line_spread(): pl.pallas_call(functools.partial(line_spread_kernel, dp, parts), out_shap...  42.7 us
    pallas_call x1, Pallas kernels, gather_update(): pl.pallas_call(functools.partial(gather_kernel, ch, rate), out_shape=jax....  40.8 us
    pallas_call x1, Pallas kernels, plane_sum(): pl.pallas_call(plane_sum_kernel, out_shape=(jax.ShapeDtypeStruct(partial....  21.1 us
    dot_general x17, matrix products, dot(): lax.dot_general(left, right, (dims, ((), ())), precision=precision, prefe...  13.4 us
    unnamed x38, local copies, waits for them, and re-layouts  11.7 us

profile of v4, /device:TPU:0, one launch (start us, length us, event | category | flops | bytes accessed | tf_op | source)
XLA Modules:
  0.0 204.7 jit_solution(4669815912111056534)
XLA Ops:
  0.7 2.4 %copy-done.4 = f32[1,2,896,608]{2,3,1,0:T(8,128)S(1)} copy-done((f32[1,2,896,608]{2,3,1,0:T(8,128)S(1)}, f32[1,2,896,608]{2,3,1,0:T(8,128)}, u32[]{:S(2)}) %copy-start.4) | copy-done | bytes 4358168
  3.0 0.7 copy-done.9
  3.7 62.2 %shard_map.144 = (f32[608,896]{1,0:T(8,128)S(1)}, f32[1,896]{1,0:T(1,128)S(1)}, f32[8,128]{1,0:T(8,128)S(1)}) custom-call(f32[2,608,896]{2,1,0:T(8,128)S(1)} %bitcast.45, f32[1,896]{1,0:T(1,128)S(1)} %copy-done.9), custom_call_target="tpu_custom_call" | custom-call | tf_op jit(solution)/shard_map/pallas_call | solution.py:144
  65.9 1.3 copy-done.1
  67.3 0.6 copy-done.8
  67.9 2.9 %fusion.8 = f32[608,256]{1,0:T(8,128)S(1)} fusion(f32[608,896]{1,0:T(8,128)} %copy-done.1, f32[2,896,256]{2,1,0:T(8,128)S(1)} %copy-done, s32[]{:T(128)S(6)} %select_n.9), kind=kOutput, calls=%fused_computation.11 | convolution fusion | flops 836763648 | bytes 3719172 | tf_op jit(solution)/shard_map/dot_general | solution.py:29
  70.8 3.0 %fusion.108.x_ref = f32[896,256]{1,0:T(8,128)} fusion(f32[608,896]{1,0:T(8,128)S(1)} %copy-done.2, f32[608,256]{1,0:T(8,128)S(1)} %fusion.8), kind=kOutput, calls=%fused_computation.121 | convolution fusion | flops 836763648 | bytes 3719168 | tf_op jit(solution)/shard_map/dot_general | solution.py:29
  73.8 21.1 %shard_map.145 = (f32[896,256]{1,0:T(8,128)}, f32[8,128]{1,0:T(8,128)}) custom-call(f32[896,256]{1,0:T(8,128)} %fusion.108.x_ref, f32[8,128]{1,0:T(8,128)} %copy-done.8), custom_call_target="tpu_custom_call" | custom-call | tf_op jit(solution)/shard_map/pallas_call | solution.py:359
  94.8 2.0 multiply_reduce_fusion
  97.5 2.4 %fusion.16 = f32[256,256]{1,0:T(8,128)S(1)} fusion(f32[896,256]{1,0:T(8,128)} %get-tuple-element.17, f32[]{:T(128)S(6)} %add.44), kind=kOutput, calls=%fused_computation.25 | convolution fusion | flops 352550912 | bytes 1179652 | tf_op jit(solution)/shard_map/dot_general | solution.py:29
  100.2 0.3 fusion.21
  100.5 0.3 fusion.20
  101.1 0.3 fusion.23
  101.4 0.3 fusion.27
  102.0 0.3 fusion.25
  102.3 0.3 fusion.19
  102.9 0.3 fusion.7
  103.5 0.3 copy-done.12
  103.8 0.5 fusion.15.refs_2_
  104.3 1.1 copy-done.3
  105.4 1.2 fusion.110.refs_0_
  106.6 42.7 %shard_map.146 = (f32[2,608,256]{2,1,0:T(8,128)S(1)}, f32[2,8,128]{2,1,0:T(8,128)S(1)}, f32[2,896,256]{2,1,0:T(8,128)S(1)}) custom-call(f32[608,256]{1,0:T(8,128)S(1)} %fusion.110.refs_0_, f32[8,128]{1,0:T(8,128)S(1)} %copy-done.7, f32[896,256]{1,0:T(8,128)S(1)} %fusion.15.refs_2_), custom_call_target="tpu_custom_call" | custom-call | tf_op jit(solution)/shard_map/pallas_call | solution.py:264
  149.3 1.2 copy-done.5
  150.5 0.5 fusion.107
  152.3 0.6 multiply_reduce_fusion.2
  153.7 3.6 %fusion.1.delta_ref = f32[2,224,608]{2,1,0:T(8,128)S(1)} fusion(f32[2,896,256]{2,1,0:T(8,128)} %copy-done.5, s32[]{:T(128)S(6)} %select_n.10, f32[2,256,608]{1,2,0:T(8,128)} %param.12, f32[2,608,256]{2,1,0:T(8,128)S(1)} %get-tuple-element.22, f32[]{:T(128)S(6)} %min_shard_map.3, f32[2,256,608]{1,2,0:T(8,128)} %param.13), kind=kOutput, calls=%fused_computation.3 | convolution fusion | flops 422117376 | bytes 5283848 | tf_op jit(solution)/shard_map/dot_general | solution.py:539
  157.3 40.8 %shard_map.147 = f32[2,224,2432]{2,1,0:T(8,128)S(1)} custom-call(f32[2,224,608]{2,1,0:T(8,128)S(1)} %fusion.1.delta_ref, f32[2,224,2432]{2,1,0:T(8,128)S(1)} %bitcast.44), custom_call_target="tpu_custom_call" | custom-call | tf_op jit(solution)/shard_map/pallas_call | solution.py:465
  198.2 1.8 fusion.28
  200.1 0.6 divide_subtract_fusion
  200.7 2.1 %copy.18 = f32[2,224,2432]{2,1,0:T(8,128)} copy(f32[2,224,2432]{2,1,0:T(8,128)S(1)} %shard_map.147) | data formatting | bytes 8716288
  202.8 0.7 copy-done.6
  203.5 1.2 copy.19
  (35 shorter events, 1.5 us)
Async XLA Ops:
  0.6 67.2 %copy-start = (f32[2,896,256]{2,1,0:T(8,128)S(1)}, f32[2,896,256]{2,1,0:T(8,128)}, u32[]{:S(2)}) copy-start(f32[2,896,256]{2,1,0:T(8,128)} %param.11) | copy-start | bytes 5505028
  0.6 2.4 %copy-start.4 = (f32[1,2,896,608]{2,3,1,0:T(8,128)S(1)}, f32[1,2,896,608]{2,3,1,0:T(8,128)}, u32[]{:S(2)}) copy-start(f32[1,2,896,608]{2,3,1,0:T(8,128)} %param.10) | copy-start | bytes 13074436
  3.0 0.7 copy-start.9
  65.9 1.3 copy-start.1
  67.3 0.6 copy-start.8
  67.9 2.9 %copy-start.2 = (f32[608,896]{1,0:T(8,128)S(1)}, f32[608,896]{1,0:T(8,128)}, u32[]{:S(2)}) copy-start(f32[608,896]{1,0:T(8,128)} %copy-done.1) | copy-start | bytes 6537220
  102.6 1.2 copy-start.12
  103.8 1.6 copy-start.3
  105.4 1.2 copy-start.7
  106.6 50.7 %slice-start = ((s8[4358144]{0:T(1024)(128)(4,1)}), s8[163840]{0:T(1024)(128)(4,1)S(1)}, s32[]{:S(2)}) async-start(s8[4358144]{0:T(1024)(128)(4,1)} %bitcast.43), calls=%async_computation | async-start | bytes 327680
  149.3 1.2 copy-start.5
  153.7 3.6 %slice-start.1 = ((s8[4358144]{0:T(1024)(128)(4,1)}), s8[4194304]{0:T(1024)(128)(4,1)S(1)}, s32[]{:S(2)}) async-start(s8[4358144]{0:T(1024)(128)(4,1)} %bitcast.43), calls=%async_computation.1 | async-start | bytes 8388608
  157.3 40.9 %copy-start.10 = (f32[2,256,608]{1,2,0:T(8,128)S(1)}, f32[2,256,608]{1,2,0:T(8,128)}, u32[]{:S(2)}) copy-start(f32[2,256,608]{1,2,0:T(8,128)} %param.12) | copy-start | bytes 3735556
  157.3 40.9 %copy-start.11 = (f32[2,256,608]{1,2,0:T(8,128)S(1)}, f32[2,256,608]{1,2,0:T(8,128)}, u32[]{:S(2)}) copy-start(f32[2,256,608]{1,2,0:T(8,128)} %param.13) | copy-start | bytes 3735556
  198.2 1.9 copy-start.13
  198.2 1.9 copy-start.14
  198.2 1.9 copy-start.15
  200.7 2.8 %copy-start.6 = (f32[2,896,256]{2,1,0:T(8,128)S(1)}, f32[2,896,256]{2,1,0:T(8,128)}, u32[]{:S(2)}) copy-start(f32[2,896,256]{2,1,0:T(8,128)} %copy-done.5) | copy-start | bytes 5505028

commit v5 on v4

--- a/solution.py
+++ b/solution.py
@@ -22,7 +22,7 @@
 MESH = pl.DeviceIdType.MESH
 VMEM = pl.BlockSpec(memory_space=pltpu.VMEM)
 SUM_SKEW = 4
-SPREAD_SKEW = 8
+SPREAD_SKEW = 2
 
 
 def dot(left, right, dims, precision=lax.Precision.HIGH):
@@ -519,7 +519,7 @@
     projected, squares, new_bases = line_spread(
         dp,
         (projected, squares, new_basis),
-        (chunk_rows(projected.shape[0], 32), 8, chunk_rows(rows // 2, 64)),
+        (chunk_rows(projected.shape[0], 152), 8, chunk_rows(rows // 2, 112)),
     )
 
     total_squares = squares[0, 0, 0] + squares[1, 0, 0] + jnp.sum(gain_total * gain_total)

time: 205 us -> 203 us (level)
  Pallas kernels: 167 us -> 164 us
    pallas_call x1, Pallas kernels: 42.7 us -> 40.3 us  [line_spread(): pl.pallas_call(functools.partial(line_spread_kernel, dp, parts), out_shap...]
where the time goes in v5:
time: 203 us; the launch traced here: 202 us
  Pallas kernels  164 us (81%)
  matrix products  16.9 us (8%)
  local copies, waits for them, and re-layouts  12.2 us (6%)
  other arithmetic  5.07 us (2%)
  between operations  3.71 us (2%)
    pallas_call x1, Pallas kernels, line_sum(): pl.pallas_call(functools.partial(line_sum_kernel, dp, ch), out_shape=(jax...  62.2 us
    pallas_call x1, Pallas kernels, gather_update(): pl.pallas_call(functools.partial(gather_kernel, ch, rate), out_shape=jax....  40.8 us
    pallas_call x1, Pallas kernels, line_spread(): pl.pallas_call(functools.partial(line_spread_kernel, dp, parts), out_shap...  40.3 us
    pallas_call x1, Pallas kernels, plane_sum(): pl.pallas_call(plane_sum_kernel, out_shape=(jax.ShapeDtypeStruct(partial....  21.1 us
    dot_general x17, matrix products, dot(): lax.dot_general(left, right, (dims, ((), ())), precision=precision, prefe...  13.4 us
    unnamed x38, local copies, waits for them, and re-layouts  11.7 us

profile of v5, /device:TPU:0, one launch (start us, length us, event | category | flops | bytes accessed | tf_op | source)
XLA Modules:
  0.0 202.3 jit_solution(7527023101820463027)
XLA Ops:
  0.7 2.4 %copy-done.4 = f32[1,2,896,608]{2,3,1,0:T(8,128)S(1)} copy-done((f32[1,2,896,608]{2,3,1,0:T(8,128)S(1)}, f32[1,2,896,608]{2,3,1,0:T(8,128)}, u32[]{:S(2)}) %copy-start.4) | copy-done | bytes 4358168
  3.0 0.7 copy-done.9
  3.7 62.2 %shard_map.144 = (f32[608,896]{1,0:T(8,128)S(1)}, f32[1,896]{1,0:T(1,128)S(1)}, f32[8,128]{1,0:T(8,128)S(1)}) custom-call(f32[2,608,896]{2,1,0:T(8,128)S(1)} %bitcast.45, f32[1,896]{1,0:T(1,128)S(1)} %copy-done.9), custom_call_target="tpu_custom_call" | custom-call | tf_op jit(solution)/shard_map/pallas_call | solution.py:144
  65.9 1.3 copy-done.1
  67.3 0.6 copy-done.8
  67.9 2.9 %fusion.8 = f32[608,256]{1,0:T(8,128)S(1)} fusion(f32[608,896]{1,0:T(8,128)} %copy-done.1, f32[2,896,256]{2,1,0:T(8,128)S(1)} %copy-done, s32[]{:T(128)S(6)} %select_n.9), kind=kOutput, calls=%fused_computation.11 | convolution fusion | flops 836763648 | bytes 3719172 | tf_op jit(solution)/shard_map/dot_general | solution.py:29
  70.8 3.0 %fusion.108.x_ref = f32[896,256]{1,0:T(8,128)} fusion(f32[608,896]{1,0:T(8,128)S(1)} %copy-done.2, f32[608,256]{1,0:T(8,128)S(1)} %fusion.8), kind=kOutput, calls=%fused_computation.121 | convolution fusion | flops 836763648 | bytes 3719168 | tf_op jit(solution)/shard_map/dot_general | solution.py:29
  73.8 21.1 %shard_map.145 = (f32[896,256]{1,0:T(8,128)}, f32[8,128]{1,0:T(8,128)}) custom-call(f32[896,256]{1,0:T(8,128)} %fusion.108.x_ref, f32[8,128]{1,0:T(8,128)} %copy-done.8), custom_call_target="tpu_custom_call" | custom-call | tf_op jit(solution)/shard_map/pallas_call | solution.py:359
  94.8 2.0 multiply_reduce_fusion
  97.5 2.4 %fusion.16 = f32[256,256]{1,0:T(8,128)S(1)} fusion(f32[896,256]{1,0:T(8,128)} %get-tuple-element.17, f32[]{:T(128)S(6)} %add.44), kind=kOutput, calls=%fused_computation.25 | convolution fusion | flops 352550912 | bytes 1179652 | tf_op jit(solution)/shard_map/dot_general | solution.py:29
  100.2 0.3 fusion.21
  100.5 0.3 fusion.20
  101.1 0.3 fusion.23
  101.4 0.3 fusion.27
  102.0 0.3 fusion.25
  102.3 0.3 fusion.19
  102.9 0.3 fusion.7
  103.5 0.3 copy-done.12
  103.8 0.5 fusion.15.refs_2_
  104.3 1.1 copy-done.3
  105.4 1.2 fusion.110.refs_0_
  106.6 40.3 %shard_map.146 = (f32[2,608,256]{2,1,0:T(8,128)S(1)}, f32[2,8,128]{2,1,0:T(8,128)S(1)}, f32[2,896,256]{2,1,0:T(8,128)S(1)}) custom-call(f32[608,256]{1,0:T(8,128)S(1)} %fusion.110.refs_0_, f32[8,128]{1,0:T(8,128)S(1)} %copy-done.7, f32[896,256]{1,0:T(8,128)S(1)} %fusion.15.refs_2_), custom_call_target="tpu_custom_call" | custom-call | tf_op jit(solution)/shard_map/pallas_call | solution.py:264
  146.9 1.2 copy-done.5
  148.1 0.5 fusion.107
  149.9 0.6 multiply_reduce_fusion.2
  151.3 3.6 %fusion.1.delta_ref = f32[2,224,608]{2,1,0:T(8,128)S(1)} fusion(f32[2,896,256]{2,1,0:T(8,128)} %copy-done.5, s32[]{:T(128)S(6)} %select_n.10, f32[2,256,608]{1,2,0:T(8,128)} %param.12, f32[2,608,256]{2,1,0:T(8,128)S(1)} %get-tuple-element.22, f32[]{:T(128)S(6)} %min_shard_map.3, f32[2,256,608]{1,2,0:T(8,128)} %param.13), kind=kOutput, calls=%fused_computation.3 | convolution fusion | flops 422117376 | bytes 5283848 | tf_op jit(solution)/shard_map/dot_general | solution.py:539
  154.9 40.8 %shard_map.147 = f32[2,224,2432]{2,1,0:T(8,128)S(1)} custom-call(f32[2,224,608]{2,1,0:T(8,128)S(1)} %fusion.1.delta_ref, f32[2,224,2432]{2,1,0:T(8,128)S(1)} %bitcast.44), custom_call_target="tpu_custom_call" | custom-call | tf_op jit(solution)/shard_map/pallas_call | solution.py:465
  195.8 1.8 fusion.28
  197.7 0.6 divide_subtract_fusion
  198.3 2.1 %copy.18 = f32[2,224,2432]{2,1,0:T(8,128)} copy(f32[2,224,2432]{2,1,0:T(8,128)S(1)} %shard_map.147) | data formatting | bytes 8716288
  200.4 0.7 copy-done.6
  201.1 1.2 copy.19
  (35 shorter events, 1.5 us)
Async XLA Ops:
  0.6 67.2 %copy-start = (f32[2,896,256]{2,1,0:T(8,128)S(1)}, f32[2,896,256]{2,1,0:T(8,128)}, u32[]{:S(2)}) copy-start(f32[2,896,256]{2,1,0:T(8,128)} %param.11) | copy-start | bytes 5505028
  0.6 2.4 %copy-start.4 = (f32[1,2,896,608]{2,3,1,0:T(8,128)S(1)}, f32[1,2,896,608]{2,3,1,0:T(8,128)}, u32[]{:S(2)}) copy-start(f32[1,2,896,608]{2,3,1,0:T(8,128)} %param.10) | copy-start | bytes 13074436
  3.0 0.7 copy-start.9
  65.9 1.3 copy-start.1
  67.3 0.6 copy-start.8
  67.9 2.9 %copy-start.2 = (f32[608,896]{1,0:T(8,128)S(1)}, f32[608,896]{1,0:T(8,128)}, u32[]{:S(2)}) copy-start(f32[608,896]{1,0:T(8,128)} %copy-done.1) | copy-start | bytes 6537220
  102.6 1.2 copy-start.12
  103.8 1.6 copy-start.3
  105.4 1.2 copy-start.7
  106.6 48.3 %slice-start = ((s8[4358144]{0:T(1024)(128)(4,1)}), s8[163840]{0:T(1024)(128)(4,1)S(1)}, s32[]{:S(2)}) async-start(s8[4358144]{0:T(1024)(128)(4,1)} %bitcast.43), calls=%async_computation | async-start | bytes 327680
  146.9 1.2 copy-start.5
  151.3 3.6 %slice-start.1 = ((s8[4358144]{0:T(1024)(128)(4,1)}), s8[4194304]{0:T(1024)(128)(4,1)S(1)}, s32[]{:S(2)}) async-start(s8[4358144]{0:T(1024)(128)(4,1)} %bitcast.43), calls=%async_computation.1 | async-start | bytes 8388608
  154.9 40.9 %copy-start.10 = (f32[2,256,608]{1,2,0:T(8,128)S(1)}, f32[2,256,608]{1,2,0:T(8,128)}, u32[]{:S(2)}) copy-start(f32[2,256,608]{1,2,0:T(8,128)} %param.12) | copy-start | bytes 3735556
  154.9 40.9 %copy-start.11 = (f32[2,256,608]{1,2,0:T(8,128)S(1)}, f32[2,256,608]{1,2,0:T(8,128)}, u32[]{:S(2)}) copy-start(f32[2,256,608]{1,2,0:T(8,128)} %param.13) | copy-start | bytes 3735556
  195.8 1.9 copy-start.13
  195.8 1.9 copy-start.14
  195.8 1.9 copy-start.15
  198.3 2.8 %copy-start.6 = (f32[2,896,256]{2,1,0:T(8,128)S(1)}, f32[2,896,256]{2,1,0:T(8,128)}, u32[]{:S(2)}) copy-start(f32[2,896,256]{2,1,0:T(8,128)} %copy-done.5) | copy-start | bytes 5505028
